TPU v7x, 32 devices: a whole 2x2x4 slice. The times are simulated.
32 devices in a mesh: cluster: 4 (over z), vector: 2 (over y), replica: 4 (over x, core).
Axes of the slice: x: 2, y: 2, z: 4, core: 2. Of those that a mesh axis runs over, the one named last changes fastest.
Arguments:
- samples: bfloat16 [128, 131072], P('vector', ('cluster', 'replica')), may hold values from -6 to 6
- leaf_basis_matrix: bfloat16 [32, 64, 2048], P(None, None, ('cluster', 'replica')), may hold values from -0.75 to 0.75
- transfer: bfloat16 [32, 32, 2048], P(None, None, ('cluster', 'replica')), may hold values from -0.75 to 0.75
- leaf_lists: int32 [4, 2048], P(None, ('cluster', 'replica')), may hold values from 0 to 2047, as said below
- leaf_coupling: bfloat16 [32, 32, 4, 2048], P(None, None, None, ('cluster', 'replica')), may hold values from -0.5 to 0.5
- parent_lists: int32 [4, 1024], P(None, ('cluster', 'replica')), may hold values from 0 to 1023, as said below
- parent_coupling: bfloat16 [32, 32, 4, 1024], P(None, None, None, ('cluster', 'replica')), may hold values from -0.5 to 0.5
- test_matrix: bfloat16 [128, 32], P('vector'), may hold values from -0.5 to 0.5
Outputs:
- product: bfloat16 [128, 131072], P('vector', ('cluster', 'replica'))
- new_basis: float32 [64, 32, 2048], P(None, None, ('cluster', 'replica'))
- fresh_transfer_sketch: float32 [32, 32, 2048], P(None, None, ('cluster', 'replica'))
Inputs may be any that keep to these rules, and one draw needn't show every extreme that they name: `leaf_lists`: every source leaf lies within 128 leaves of its target leaf, and some source lies exactly 128 leaves away. `parent_lists`: every source parent lies within half of 128 parents of its target parent, and some source lies exactly that far away.
All inputs are finite; a program needn't handle non-finite values.
Results may differ from a plain program's by a relative error of at most 0.0062.
Values may be sent and summed in bfloat16 or wider, within the bound.
A program may use at most 64 MiB of HBM per device.

v0:
```python
import jax
import jax.numpy as jnp
from jax import lax
from jax.sharding import PartitionSpec as P


def extended_2(block, sides, width):
    for axis, dim in sides:
        count = lax.axis_size(axis)
        forward = [(i, i + 1) for i in range(count - 1)]
        backward = [(target, source) for source, target in forward]
        low = lax.ppermute(
            lax.slice_in_dim(block, block.shape[dim] - width, None, axis=dim), axis, forward
        )
        high = lax.ppermute(lax.slice_in_dim(block, 0, width, axis=dim), axis, backward)
        block = jnp.concatenate([low, block, high], axis=dim)
    return block


def finish_basis(sketch, width):
    scale = lax.rsqrt(jnp.mean(sketch * sketch, axis=0, keepdims=True) + 1e-06)
    new_basis = sketch * scale
    fresh_transfer_sketch = (
        jnp.einsum("pal,pbl->abl", new_basis, sketch, precision=lax.Precision.HIGHEST) / width
    )
    return (new_basis, fresh_transfer_sketch)


def near_take(extended, lists, count):
    first = lax.axis_index(("cluster", "replica")) * count - count
    local_index = lists - first
    return jnp.take(extended, local_index, axis=2)


def shards(
    samples,
    leaf_basis_matrix,
    transfer,
    leaf_lists,
    leaf_coupling,
    parent_lists,
    parent_coupling,
    test_matrix,
):
    rank, width, leaves = leaf_basis_matrix.shape
    vec_local = samples.shape[0]
    each_leaf_amount = samples.reshape(vec_local, leaves, width)
    leaf_coeff = jnp.einsum(
        "rpl,vlp->rvl", leaf_basis_matrix, each_leaf_amount, preferred_element_type=jnp.float32
    ).astype(jnp.bfloat16)
    pairs = transfer.reshape(rank, rank, leaves // 2, 2)
    children = leaf_coeff.reshape(rank, vec_local, leaves // 2, 2)
    parent_coeff = jnp.einsum(
        "abqc,avqc->bvq", pairs, children, preferred_element_type=jnp.float32
    ).astype(jnp.bfloat16)
    leaf_ext = extended_2(leaf_coeff, ((("cluster", "replica"), 2),), leaves)
    leaf_src = near_take(leaf_ext, leaf_lists, leaves)
    parent_ext = extended_2(parent_coeff, ((("cluster", "replica"), 2),), leaves // 2)
    parent_src = near_take(parent_ext, parent_lists, leaves // 2)
    leaf_far = jnp.einsum(
        "rskt,svkt->rvt", leaf_coupling, leaf_src, preferred_element_type=jnp.float32
    )
    parent_far = jnp.einsum(
        "rskq,svkq->rvq", parent_coupling, parent_src, preferred_element_type=jnp.float32
    )
    descend = jnp.einsum(
        "abqc,bvq->avqc", pairs.astype(jnp.float32), parent_far, precision=lax.Precision.HIGHEST
    )
    leaf_count_total = (leaf_far + descend.reshape(rank, vec_local, leaves)).astype(jnp.bfloat16)
    product = jnp.einsum(
        "etw,ebw->bwt", leaf_basis_matrix, leaf_count_total, preferred_element_type=jnp.float32
    ).astype(jnp.bfloat16)
    partial_sketch = jnp.einsum(
        "vlp,vr->prl", product, test_matrix, preferred_element_type=jnp.float32
    )
    sketch = lax.psum(partial_sketch, "vector")
    new_basis, fresh_transfer_sketch = finish_basis(sketch, width)
    return (product.reshape(vec_local, leaves * width), new_basis, fresh_transfer_sketch)


def solution(mesh):
    placed = (
        P("vector", ("cluster", "replica")),
        P(None, None, ("cluster", "replica")),
        P(None, None, ("cluster", "replica")),
        P(None, ("cluster", "replica")),
        P(None, None, None, ("cluster", "replica")),
        P(None, ("cluster", "replica")),
        P(None, None, None, ("cluster", "replica")),
        P("vector", None),
    )
    return jax.shard_map(
        shards,
        mesh=mesh,
        in_specs=placed,
        out_specs=(
            P("vector", ("cluster", "replica")),
            P(None, None, ("cluster", "replica")),
            P(None, None, ("cluster", "replica")),
        ),
        check_vma=False,
    )
```

profile of v0, /device:TPU:1, one launch (start us, length us, event | category | flops | bytes accessed | tf_op | source)
XLA Modules:
  0.0 145.1 jit_solution(2610719103954319102)
XLA Ops:
  7.2 2.5 %copy.31 = bf16[32,64,128]{1,0,2:T(8,128)(2,1)S(1)} copy(bf16[32,64,128]{2,1,0:T(8,128)(2,1)} %param.9) | data formatting | bytes 1048576 | tf_op args[1]
  9.8 3.3 %reshape.39 = bf16[64,128,64]{2,1,0:T(8,128)(2,1)} reshape(bf16[64,8192]{1,0:T(8,128)(2,1)S(1)} %copy-done.6) | data formatting | bytes 2097152 | tf_op jit(solution)/shard_map/reshape | solution.py:47
  13.1 3.2 %fusion.12 = bf16[128,64,32]{1,2,0:T(8,128)(2,1)S(1)} fusion(bf16[32,64,128]{1,0,2:T(8,128)(2,1)S(1)} %copy.31, bf16[64,128,64]{2,1,0:T(8,128)(2,1)} %reshape.39), kind=kOutput, calls=%fused_computation.19 | convolution fusion | flops 33816576 | bytes 2097152 | tf_op jit(solution)/shard_map/rpl,vlp->rvl/dot_general | solution.py:48
  16.3 1.1 copy.32
  17.4 1.9 %collective-permute-start.1 = (bf16[32,64,128]{2,1,0:T(8,128)(2,1)S(1)}, bf16[32,64,128]{2,1,0:T(8,128)(2,1)}, u32[]{:S(2)}, u32[]{:S(2)}) collective-permute-start(bf16[32,64,128]{2,1,0:T(8,128)(2,1)S(1)} %copy.32), channel_id=1, source_target_pairs={{1,0},{2,1},{3,2},{8,3},{9,8},{10,9},{11,10},{16,11},{17,16},{18,1... | collective-permute-start | bytes 1572872 | tf_op jit(solution)/shard_map/ppermute | solution.py:15
  19.4 4.5 %collective-permute-start = (bf16[32,64,128]{2,1,0:T(8,128)(2,1)S(1)}, bf16[32,64,128]{2,1,0:T(8,128)(2,1)}, u32[]{:S(2)}, u32[]{:S(2)}) collective-permute-start(bf16[32,64,128]{2,1,0:T(8,128)(2,1)S(1)} %copy.32), channel_id=1, source_target_pairs={{0,1},{1,2},{2,3},{3,8},{8,9},{9,10},{10,11},{11,16},{16,17},{17,1... | collective-permute-start | bytes 1572872 | tf_op jit(solution)/shard_map/ppermute | solution.py:12
  23.9 1.4 copy.50
  25.8 1.9 %collective-permute-start.3 = (bf16[32,64,64]{1,0,2:T(8,128)(2,1)S(1)}, bf16[32,64,64]{1,0,2:T(8,128)(2,1)}, u32[]{:S(2)}, u32[]{:S(2)}) collective-permute-start(bf16[32,64,64]{1,0,2:T(8,128)(2,1)S(1)} %fusion.21), channel_id=1, source_target_pairs={{1,0},{2,1},{3,2},{8,3},{9,8},{10,9},{11,10},{16,11},{17,16},{18,1... | collective-permute-start | bytes 786440 | tf_op jit(solution)/shard_map/ppermute | solution.py:15
  27.7 3.8 %collective-permute-start.2 = (bf16[32,64,64]{1,0,2:T(8,128)(2,1)S(1)}, bf16[32,64,64]{1,0,2:T(8,128)(2,1)}, u32[]{:S(2)}, u32[]{:S(2)}) collective-permute-start(bf16[32,64,64]{1,0,2:T(8,128)(2,1)S(1)} %fusion.21), channel_id=1, source_target_pairs={{0,1},{1,2},{2,3},{3,8},{8,9},{9,10},{10,11},{11,16},{16,17},{17,1... | collective-permute-start | bytes 786440 | tf_op jit(solution)/shard_map/ppermute | solution.py:12
  31.7 4.4 %copy.39 = bf16[32,32,4,64]{1,0,3,2:T(8,128)(2,1)} copy(bf16[32,32,4,64]{3,2,1,0:T(4,128)(2,1)} %param.14) | data formatting | bytes 1048576 | tf_op args[6]
  36.1 5.4 %copy.36 = bf16[32,32,4,128]{1,0,3,2:T(8,128)(2,1)} copy(bf16[32,32,4,128]{3,2,1,0:T(4,128)(2,1)} %param.12) | data formatting | bytes 2097152 | tf_op args[4]
  41.5 4.3 %collective-permute-done.2 = bf16[32,64,64]{1,0,2:T(8,128)(2,1)} collective-permute-done((bf16[32,64,64]{1,0,2:T(8,128)(2,1)S(1)}, bf16[32,64,64]{1,0,2:T(8,128)(2,1)}, u32[]{:S(2)}, u32[]{:S(2)}) %collective-permute-start.2) | collective-permute-done | bytes 262176 | tf_op jit(solution)/shard_map/ppermute | solution.py:12
  45.8 2.7 %pad_maximum_fusion.1 = bf16[32,64,192]{1,0,2:T(8,128)(2,1)} fusion(bf16[32,64,64]{1,0,2:T(8,128)(2,1)} %collective-permute-done.3, bf16[32,64,64]{1,0,2:T(8,128)(2,1)S(1)} %fusion.21, bf16[32,64,64]{1,0,2:T(8,128)(2,1)} %collective-permute-done.2), kind=kLoop, calls=%fused_computation.18 | loop fusion | flops 786432 | bytes 1572864 | tf_op jit(solution)/shard_map/concatenate | solution.py:16
  48.5 3.6 %gather_fusion.1 = bf16[256,32,64]{2,1,0:T(8,128)(2,1)} fusion(bf16[32,64,192]{1,0,2:T(8,128)(2,1)} %pad_maximum_fusion.1, s32[1024]{0:T(1024)S(1)} %pad_clamp_fusion), kind=kCustom, calls=%fused_computation.1 | custom fusion | bytes 2098176 | tf_op jit(solution)/shard_map/jit(_take)/gather | solution.py:32
  52.1 3.1 %fusion.17 = f32[32,64,64,1]{1,0,3,2:T(8,128)S(1)} fusion(bf16[32,32,4,64]{1,0,3,2:T(8,128)(2,1)} %copy.39, bf16[4,64,32,64]{3,2,1,0:T(8,128)(2,1)} %bitcast.73, pred[4,64]{1,0:T(4,128)(4,1)S(1)} %get-tuple-element.12), kind=kOutput, calls=%fused_computation.20 | convolution fusion | flops 34078720 | bytes 2097408 | tf_op jit(solution)/shard_map/rskq,svkq->rvq/dot_general | solution.py:63
  55.2 2.4 %fusion.27 = f32[64,64,32,2]{1,2,3,0:T(8,128)} fusion(f32[32,64,64,1]{1,0,3,2:T(8,128)S(1)} %fusion.17, bf16[32,32,64,2]{1,0,3,2:T(8,128)(2,1)S(1)} %bitcast.72), kind=kOutput, calls=%fused_computation.39 | convolution fusion | flops 100663296 | bytes 1835008 | tf_op jit(solution)/shard_map/abqc,bvq->avqc/dot_general | solution.py:66
  57.7 2.5 %copy.35 = bf16[32,64,128]{1,0,2:T(8,128)(2,1)S(1)} copy(bf16[32,64,128]{2,1,0:T(8,128)(2,1)} %collective-permute-done.1) | data formatting | bytes 1048576 | tf_op jit(solution)/shard_map/ppermute | solution.py:15
  60.2 2.5 %copy.34 = bf16[32,64,128]{1,0,2:T(8,128)(2,1)S(1)} copy(bf16[32,64,128]{2,1,0:T(8,128)(2,1)} %collective-permute-done) | data formatting | bytes 1048576 | tf_op jit(solution)/shard_map/ppermute | solution.py:12
  62.6 2.1 %pad_maximum_fusion = bf16[32,64,384]{1,0,2:T(8,128)(2,1)} fusion(bf16[32,64,128]{1,0,2:T(8,128)(2,1)S(1)} %copy.35, bf16[32,64,128]{1,0,2:T(8,128)(2,1)S(1)} %bitcast.70, bf16[32,64,128]{1,0,2:T(8,128)(2,1)S(1)} %copy.34), kind=kLoop, calls=%fused_computation.6 | loop fusion | flops 1572864 | bytes 3145728 | tf_op jit(solution)/shard_map/concatenate | solution.py:16
  64.7 5.2 %gather_fusion = bf16[512,32,64]{2,1,0:T(8,128)(2,1)} fusion(bf16[32,64,384]{1,0,2:T(8,128)(2,1)} %pad_maximum_fusion, s32[1024]{0:T(1024)S(1)} %pad_clamp_fusion.1), kind=kCustom, calls=%fused_computation | custom fusion | bytes 4196352 | tf_op jit(solution)/shard_map/jit(_take)/gather | solution.py:32
  69.9 5.3 %fusion.4 = bf16[32,64,128]{1,0,2:T(8,128)(2,1)S(1)} fusion(f32[64,64,32,2]{1,2,3,0:T(8,128)S(1)} %copy-done.5, bf16[32,32,4,128]{1,0,3,2:T(8,128)(2,1)} %copy.36, bf16[4,128,32,64]{3,2,1,0:T(8,128)(2,1)} %bitcast.74, pred[4,128]{1,0:T(4,128)(4,1)S(1)} %compare_and_fusion.1), kind=kOutput, calls=%fused_computation.8 | convolution fusion | flops 68681728 | bytes 4719104 | tf_op jit(solution)/shard_map/rskt,svkt->rvt/dot_general | solution.py:60
  76.0 3.4 %copy.42 = bf16[64,128,64]{1,0,2:T(8,128)(2,1)S(1)} copy(bf16[64,128,64]{2,0,1:T(8,128)(2,1)S(1)} %convert_bitcast_fusion) | data formatting | bytes 2097152 | tf_op jit(solution)/shard_map/convert_element_type | solution.py:72
  79.3 1.3 convolution_bitcast_fusion
  80.6 2.7 %copy.41 = bf16[64,128,64]{2,1,0:T(8,128)(2,1)} copy(bf16[64,128,64]{2,0,1:T(8,128)(2,1)S(1)} %convert_bitcast_fusion) | data formatting | bytes 2097152 | tf_op jit(solution)/shard_map/convert_element_type | solution.py:72
  83.3 4.1 %reshape.43 = bf16[64,8192]{1,0:T(8,128)(2,1)} reshape(bf16[64,128,64]{2,1,0:T(8,128)(2,1)} %copy.41) | data formatting | bytes 2097152 | tf_op jit(solution)/shard_map/reshape | solution.py:78
  87.4 34.3 %all-reduce.2.cloned.1.call-done = f32[64,32,128]{2,1,0:T(8,128)} async-done(((f32[64,32,128]{2,1,0:T(8,128)}), f32[64,32,128]{2,1,0:T(8,128)}) %all-reduce.2.cloned.1.call-update) | async-done | bytes 1048592 | tf_op jit(solution)/shard_map/psum | solution.py:76
  121.8 1.3 multiply_reduce_fusion
  123.1 1.3 broadcast_multiply_fusion
  124.4 2.9 %copy.44 = f32[64,32,128]{0,1,2:T(8,128)} copy(f32[64,32,128]{2,1,0:T(8,128)S(1)} %broadcast_multiply_fusion) | data formatting | bytes 2097152 | tf_op jit(solution)/shard_map/mul | solution.py:22
  127.4 2.9 %copy.43 = f32[64,32,128]{0,1,2:T(8,128)} copy(f32[64,32,128]{2,1,0:T(8,128)S(1)} %copy-done.1) | data formatting | bytes 2097152 | tf_op jit(solution)/shard_map/psum | solution.py:76
  130.3 5.7 %multiply_bitcast_fusion = f32[32,32,128]{0,1,2:T(8,128)S(1)} fusion(f32[64,32,128]{0,1,2:T(8,128)} %copy.43, f32[64,32,128]{0,1,2:T(8,128)} %copy.44), kind=kOutput, calls=%fused_computation.15 | convolution fusion | flops 100794368 | bytes 2621440 | tf_op jit(solution)/shard_map/pal,pbl->abl/dot_general | solution.py:24
  136.0 2.2 %copy.45 = f32[32,32,128]{2,1,0:T(8,128)} copy(f32[32,32,128]{0,1,2:T(8,128)S(1)} %multiply_bitcast_fusion) | data formatting | bytes 1048576
  (34 shorter events, 1.5 us)
Async XLA Ops:
  7.2 72.2 %copy-start = (bf16[64,32]{0,1:T(8,128)(2,1)S(1)}, bf16[64,32]{0,1:T(8,128)(2,1)}, u32[]{:S(2)}) copy-start(bf16[64,32]{0,1:T(8,128)(2,1)} %param.15) | copy-start | bytes 12292
  7.2 2.6 %copy-start.6 = (bf16[64,8192]{1,0:T(8,128)(2,1)S(1)}, bf16[64,8192]{1,0:T(8,128)(2,1)}, u32[]{:S(2)}) copy-start(bf16[64,8192]{1,0:T(8,128)(2,1)} %param.8) | copy-start | bytes 3145732
  7.2 114.6 %all-reduce.2.cloned.1.call-start = ((), (), s32[]{:S(2)}) async-start(), calls=%async_computation | async-start | bytes 2097152 | tf_op jit(solution)/shard_map/psum | solution.py:76
  9.8 6.5 %copy-start.2 = (bf16[32,64,128]{1,0,2:T(8,128)(2,1)}, bf16[32,64,128]{1,0,2:T(8,128)(2,1)S(1)}, u32[]{:S(2)}) copy-start(bf16[32,64,128]{1,0,2:T(8,128)(2,1)S(1)} %copy.31) | copy-start | bytes 1572868
  13.1 10.8 %copy-start.7 = (bf16[32,32,128]{2,1,0:T(8,128)(2,1)S(1)}, bf16[32,32,128]{2,1,0:T(8,128)(2,1)}, u32[]{:S(2)}) copy-start(bf16[32,32,128]{2,1,0:T(8,128)(2,1)} %param.10) | copy-start | bytes 786436
  17.4 14.2 %copy-start.8 = (s32[4,128]{1,0:T(4,128)S(1)}, s32[4,128]{1,0:T(4,128)}, u32[]{:S(2)}) copy-start(s32[4,128]{1,0:T(4,128)} %param.11) | copy-start | bytes 6148
  17.4 14.2 %copy-start.9 = (s32[4,64]{1,0:T(4,128)S(1)}, s32[4,64]{1,0:T(4,128)}, u32[]{:S(2)}) copy-start(s32[4,64]{1,0:T(4,128)} %param.13) | copy-start | bytes 3076
  17.4 40.3 %collective-permute-start.1 = (bf16[32,64,128]{2,1,0:T(8,128)(2,1)S(1)}, bf16[32,64,128]{2,1,0:T(8,128)(2,1)}, u32[]{:S(2)}, u32[]{:S(2)}) collective-permute-start(bf16[32,64,128]{2,1,0:T(8,128)(2,1)S(1)} %copy.32), channel_id=1, source_target_pairs={{1,0},{2,1},{3,2},{8,3},{9,8},{10,9},{11,10},{16,11},{17,16},{18,1... | collective-permute-start | bytes 1572872 | tf_op jit(solution)/shard_map/ppermute | solution.py:15
  19.4 40.8 %collective-permute-start = (bf16[32,64,128]{2,1,0:T(8,128)(2,1)S(1)}, bf16[32,64,128]{2,1,0:T(8,128)(2,1)}, u32[]{:S(2)}, u32[]{:S(2)}) collective-permute-start(bf16[32,64,128]{2,1,0:T(8,128)(2,1)S(1)} %copy.32), channel_id=1, source_target_pairs={{0,1},{1,2},{2,3},{3,8},{8,9},{9,10},{10,11},{11,16},{16,17},{17,1... | collective-permute-start | bytes 1572872 | tf_op jit(solution)/shard_map/ppermute | solution.py:12
  25.8 15.7 %collective-permute-start.3 = (bf16[32,64,64]{1,0,2:T(8,128)(2,1)S(1)}, bf16[32,64,64]{1,0,2:T(8,128)(2,1)}, u32[]{:S(2)}, u32[]{:S(2)}) collective-permute-start(bf16[32,64,64]{1,0,2:T(8,128)(2,1)S(1)} %fusion.21), channel_id=1, source_target_pairs={{1,0},{2,1},{3,2},{8,3},{9,8},{10,9},{11,10},{16,11},{17,16},{18,1... | collective-permute-start | bytes 786440 | tf_op jit(solution)/shard_map/ppermute | solution.py:15
  27.7 18.1 %collective-permute-start.2 = (bf16[32,64,64]{1,0,2:T(8,128)(2,1)S(1)}, bf16[32,64,64]{1,0,2:T(8,128)(2,1)}, u32[]{:S(2)}, u32[]{:S(2)}) collective-permute-start(bf16[32,64,64]{1,0,2:T(8,128)(2,1)S(1)} %fusion.21), channel_id=1, source_target_pairs={{0,1},{1,2},{2,3},{3,8},{8,9},{9,10},{10,11},{11,16},{16,17},{17,1... | collective-permute-start | bytes 786440 | tf_op jit(solution)/shard_map/ppermute | solution.py:12
  64.7 5.2 %copy-start.5 = (f32[64,64,32,2]{1,2,3,0:T(8,128)S(1)}, f32[64,64,32,2]{1,2,3,0:T(8,128)}, u32[]{:S(2)}) copy-start(f32[64,64,32,2]{1,2,3,0:T(8,128)} %fusion.27) | copy-start | bytes 3145732
  69.9 5.3 %copy-start.3 = (bf16[32,64,128]{1,0,2:T(8,128)(2,1)S(1)}, bf16[32,64,128]{1,0,2:T(8,128)(2,1)}, u32[]{:S(2)}) copy-start(bf16[32,64,128]{1,0,2:T(8,128)(2,1)} %copy-done.2) | copy-start | bytes 1572868
  124.4 3.0 %copy-start.4 = (f32[64,32,128]{2,1,0:T(8,128)}, f32[64,32,128]{2,1,0:T(8,128)S(1)}, u32[]{:S(2)}) copy-start(f32[64,32,128]{2,1,0:T(8,128)S(1)} %broadcast_multiply_fusion) | copy-start | bytes 3145732
  124.4 3.0 %copy-start.1 = (f32[64,32,128]{2,1,0:T(8,128)S(1)}, f32[64,32,128]{2,1,0:T(8,128)}, u32[]{:S(2)}) copy-start(f32[64,32,128]{2,1,0:T(8,128)} %all-reduce.2.cloned.1.call-done) | copy-start | bytes 3145732
Sparse Core Ops, SparseCore 0:
  80.7 40.9 all-reduce.1
where the time goes:
time: 147 us; the launch traced here: 145 us
  local copies, waits for them, and re-layouts  50.3 us (34%)
  waiting for transfers between devices  38.6 us (26%)
  matrix products  22.1 us (15%)
  between operations  14.3 us (10%)
  starting transfers between devices  12.2 us (8%)
  other arithmetic  7.48 us (5%)
    psum x1, waiting for transfers between devices, shards(): sketch = lax.psum(partial_sketch, 'vector')  34.3 us
    unnamed x24, local copies, waits for them, and re-layouts  14.6 us
    gather x2, local copies, waits for them, and re-layouts, near_take(): return jnp.take(extended, local_index, axis=2)  8.81 us
    ppermute x2, starting transfers between devices, extended_2(): lax.ppermute(lax.slice_in_dim(block, block.shape[dim] - width, None, axis...  8.32 us
    convert_element_type x2, local copies, waits for them, and re-layouts, shards(): product = jnp.einsum('etw,ebw->bwt', leaf_basis_matrix, leaf_count_total,...  6.04 us
    dot_general x1, matrix products, finish_basis(): jnp.einsum('pal,pbl->abl', new_basis, sketch, precision=lax.Precision.HIG...  5.68 us
    dot_general x1, matrix products, shards(): jnp.einsum('rskt,svkt->rvt', leaf_coupling, leaf_src, preferred_element_t...  5.28 us
    concatenate x2, other arithmetic, extended_2(): block = jnp.concatenate([low, block, high], axis=dim)  4.79 us
  transfers between devices with their start and end apart: 5, of which 2 were waited for; matrix products, arithmetic and copies ran while one was open for 23% of the time, Pallas kernels for 0%

commit v1 on v0

v1 whole, which is shorter than its diff:
```python
import functools

import jax
import jax.numpy as jnp
from jax import lax
from jax.experimental import pallas as pl
from jax.experimental.pallas import tpu as pltpu
from jax.sharding import PartitionSpec as P

F32 = jnp.float32
BF16 = jnp.bfloat16
LINE = ("cluster", "replica")
TN = (((0,), (0,)), ((), ()))
NT = (((1,), (1,)), ((), ()))


def dot(a, b, dims=(((1,), (0,)), ((), ()))):
    return lax.dot_general(a, b, dims, preferred_element_type=F32)


def block_diagonal(pair):
    first, second = pair[0], pair[1]
    zero = jnp.zeros_like(first)
    return jnp.concatenate(
        [jnp.concatenate([first, zero], axis=1), jnp.concatenate([zero, second], axis=1)], axis=0
    )


def coeff_kernel(samples_ref, basis_ref, down_ref, coeff_ref):
    count, rank = down_ref.shape[0], down_ref.shape[1]
    width = 2 * basis_ref.shape[2]
    half = rank // 2
    for q in range(count):
        both = block_diagonal((basis_ref[2 * q], basis_ref[2 * q + 1]))
        points = samples_ref[:, q * width : (q + 1) * width]
        leaf = dot(both, points, NT).astype(BF16)
        parent = dot(down_ref[q], leaf).astype(BF16)
        coeff_ref[q, :rank, :] = jnp.concatenate([leaf[:rank], leaf[rank:]], axis=1)
        coeff_ref[q, rank:, :] = jnp.concatenate([parent[:half], parent[half:]], axis=1)


def swap_halves(block):
    half = block.shape[1] // 2
    return jnp.concatenate([block[:, half:], block[:, :half]], axis=1)


def far_kernel(
    leaf_lists_ref,
    parent_lists_ref,
    low_ref,
    own_ref,
    high_ref,
    leaf_coupling_ref,
    parent_coupling_ref,
    down_ref,
    basis_ref,
    test_ref,
    product_ref,
    packed_ref,
    leaf_ext,
    parent_ext,
    totals,
):
    step = pl.program_id(0)
    count, rank = down_ref.shape[0], down_ref.shape[1]
    vectors = product_ref.shape[0]
    width = 2 * basis_ref.shape[2]
    parents = own_ref.shape[0]

    @pl.when(step == 0)
    def _():
        for place, ref in enumerate((low_ref, own_ref, high_ref)):

            @pl.loop(0, parents // 4)
            def _(group):
                for u in range(4):
                    q = group * 4 + u
                    target = place * parents + q
                    pair = ref[q, :rank, :]
                    up = ref[q, rank:, :]
                    leaf_ext[2 * target] = pair
                    leaf_ext[2 * target + 1] = swap_halves(pair)
                    parent_ext[target, : rank // 2, :] = up
                    parent_ext[target, rank // 2 :, :] = swap_halves(up)

    for i in range(count):
        q = step * count + i
        far = []
        for c in range(2):
            t = 2 * q + c
            source = jnp.concatenate(
                [leaf_ext[leaf_lists_ref[k, t]] for k in range(leaf_lists_ref.shape[0])], axis=0
            )
            far.append(dot(leaf_coupling_ref[2 * i + c], source))
        source = jnp.concatenate(
            [parent_ext[parent_lists_ref[k, q]] for k in range(parent_lists_ref.shape[0])], axis=0
        )
        parent_far = dot(parent_coupling_ref[i], source).astype(BF16)
        descend = dot(down_ref[i], parent_far, TN)
        total = (jnp.concatenate(far, axis=0) + descend).astype(BF16)
        rows = pl.ds(pl.multiple_of(q * 2 * rank, 2 * rank), 2 * rank)
        totals[rows, :] = total.astype(F32)
        both = block_diagonal((basis_ref[2 * i], basis_ref[2 * i + 1]))
        product_ref[:, i * width : (i + 1) * width] = dot(total[:, :vectors], both, TN).astype(BF16)

    @pl.when(step == pl.num_programs(0) - 1)
    def _():
        for a in range(rank):
            mine = totals[pl.ds(a, 2 * parents, stride=rank), :][:, :vectors].astype(BF16)
            packed_ref[a * rank : (a + 1) * rank, :] = dot(test_ref[...], mine, (((0,), (1,)), ((), ()))).astype(BF16)


def finish_kernel(parts, *refs):
    basis_ref, new_basis_ref, fresh_ref, summed, wide, sketch = refs[parts:]
    rank, width = basis_ref.shape[0], basis_ref.shape[1]
    lanes = basis_ref.shape[2]
    total = refs[0][...].astype(F32)
    for ref in refs[1:parts]:
        total = total + ref[...].astype(F32)
    summed[...] = total
    for a in range(rank):
        wide[a * width : (a + 1) * width, :] = basis_ref[a].astype(F32)
    group = 8

    def points(block, square):
        first = block * group
        acc = [jnp.zeros((rank, lanes), F32) for _ in range(group)]
        for a in range(rank):
            mixed = summed[a * rank : (a + 1) * rank, :]
            for j in range(group):
                acc[j] = acc[j] + wide[pl.ds(a * width + first + j, 1), :] * mixed
        for j in range(group):
            sketch[first + j] = acc[j]
            square = square + acc[j] * acc[j]
        return square

    square = lax.fori_loop(0, width // group, points, jnp.zeros((rank, lanes), F32))
    scale = lax.rsqrt(square / width + 1e-06)
    for p in range(width):
        new_basis_ref[p] = sketch[p] * scale

    def grams(block, carry):
        first = block * group

        acc = [jnp.zeros((rank, lanes), F32) for _ in range(group)]
        for p in range(width):
            row = sketch[p]
            for j in range(group):
                acc[j] = acc[j] + new_basis_ref[p, pl.ds(first + j, 1), :] * row
        for j in range(group):
            fresh_ref[first + j] = acc[j] / width
        return carry

    lax.fori_loop(0, rank // group, grams, 0)


def shards(
    samples,
    leaf_basis_matrix,
    transfer,
    leaf_lists,
    leaf_coupling,
    parent_lists,
    parent_coupling,
    test_matrix,
):
    rank, width, leaves = leaf_basis_matrix.shape
    vectors = samples.shape[0]
    parents = leaves // 2
    leaf_blocks, parent_blocks = leaf_lists.shape[0], parent_lists.shape[0]
    count = 8
    steps = parents // count

    basis = leaf_basis_matrix.transpose(2, 0, 1)
    down = transfer.reshape(rank, rank, parents, 2).transpose(2, 1, 3, 0).reshape(parents, rank, 2 * rank)
    coeff = pl.pallas_call(
        coeff_kernel,
        grid=(steps,),
        in_specs=[
            pl.BlockSpec((vectors, 2 * count * width), lambda i: (0, i)),
            pl.BlockSpec((2 * count, rank, width), lambda i: (i, 0, 0)),
            pl.BlockSpec((count, rank, 2 * rank), lambda i: (i, 0, 0)),
        ],
        out_specs=pl.BlockSpec((count, rank + rank // 2, 2 * vectors), lambda i: (i, 0, 0)),
        out_shape=jax.ShapeDtypeStruct((parents, rank + rank // 2, 2 * vectors), BF16),
        name="coefficients",
    )(samples, basis, down)

    size = lax.axis_size(LINE)
    forward = [(i, i + 1) for i in range(size - 1)]
    backward = [(i + 1, i) for i in range(size - 1)]
    low = lax.ppermute(coeff, LINE, forward)
    high = lax.ppermute(coeff, LINE, backward)

    position = lax.axis_index(LINE)
    leaf_local = leaf_lists - (position - 1) * leaves
    parent_local = parent_lists - (position - 1) * parents
    leaf_mats = leaf_coupling.transpose(3, 0, 2, 1).reshape(leaves, rank, leaf_blocks * rank)
    parent_mats = parent_coupling.transpose(3, 0, 2, 1).reshape(parents, rank, parent_blocks * rank)

    whole = pl.BlockSpec(coeff.shape, lambda i, *_: (0, 0, 0))
    product, packed = pl.pallas_call(
        far_kernel,
        grid_spec=pltpu.PrefetchScalarGridSpec(
            num_scalar_prefetch=2,
            grid=(steps,),
            in_specs=[
                whole,
                whole,
                whole,
                pl.BlockSpec((2 * count, rank, leaf_blocks * rank), lambda i, *_: (i, 0, 0)),
                pl.BlockSpec((count, rank, parent_blocks * rank), lambda i, *_: (i, 0, 0)),
                pl.BlockSpec((count, rank, 2 * rank), lambda i, *_: (i, 0, 0)),
                pl.BlockSpec((2 * count, rank, width), lambda i, *_: (i, 0, 0)),
                pl.BlockSpec(test_matrix.shape, lambda i, *_: (0, 0)),
            ],
            out_specs=[
                pl.BlockSpec((vectors, 2 * count * width), lambda i, *_: (0, i)),
                pl.BlockSpec((rank * rank, leaves), lambda i, *_: (0, 0)),
            ],
            scratch_shapes=[
                pltpu.VMEM((3 * leaves, rank, 2 * vectors), BF16),
                pltpu.VMEM((3 * parents, rank, 2 * vectors), BF16),
                pltpu.VMEM((leaves * rank, 2 * vectors), F32),
            ],
        ),
        out_shape=[
            jax.ShapeDtypeStruct(samples.shape, BF16),
            jax.ShapeDtypeStruct((rank * rank, leaves), BF16),
        ],
        name="far_field",
    )(leaf_local, parent_local, low, coeff, high, leaf_mats, parent_mats, down, basis, test_matrix)

    if lax.axis_size("vector") == 2:
        pieces = (packed, lax.ppermute(packed, "vector", [(0, 1), (1, 0)]))
    else:
        pieces = (lax.psum(packed.astype(F32), "vector"),)
    new_basis, fresh = pl.pallas_call(
        functools.partial(finish_kernel, len(pieces)),
        in_specs=[pl.BlockSpec(memory_space=pltpu.VMEM)] * (len(pieces) + 1),
        out_specs=[pl.BlockSpec(memory_space=pltpu.VMEM)] * 2,
        out_shape=[
            jax.ShapeDtypeStruct((width, rank, leaves), F32),
            jax.ShapeDtypeStruct((rank, rank, leaves), F32),
        ],
        scratch_shapes=[
            pltpu.VMEM((rank * rank, leaves), F32),
            pltpu.VMEM((rank * width, leaves), F32),
            pltpu.VMEM((width, rank, leaves), F32),
        ],
        name="finish",
    )(*pieces, leaf_basis_matrix)
    return product, new_basis, fresh


def solution(mesh):
    placed = (
        P("vector", LINE),
        P(None, None, LINE),
        P(None, None, LINE),
        P(None, LINE),
        P(None, None, None, LINE),
        P(None, LINE),
        P(None, None, None, LINE),
        P("vector", None),
    )
    return jax.shard_map(
        shards,
        mesh=mesh,
        in_specs=placed,
        out_specs=(P("vector", LINE), P(None, None, LINE), P(None, None, LINE)),
        check_vma=False,
    )
```

time: 147 us -> 88.9 us (0.60)
  Pallas kernels: 0 us -> 51.6 us
  local copies, waits for them, and re-layouts: 50.3 us -> 12 us
  waiting for transfers between devices: 38.6 us -> 14.3 us
  matrix products: 22.1 us -> 0 us
  between operations: 14.3 us -> 0.72 us
  other arithmetic: 7.48 us -> 1.17 us
  starting transfers between devices: 12.2 us -> 7.71 us
    pallas_call x0 -> x3, Pallas kernels: none -> 51.6 us  [the longest x1 30.5 us: shards(): pl.pallas_call(far_kernel, grid_spec=pltpu.PrefetchScalarGridSpec(num_sca...]
    psum x1 -> x0, waiting for transfers between devices: 34.3 us -> none  [shards(): sketch = lax.psum(partial_sketch, 'vector')]
    dot_general x8 -> x0, matrix products: 22.1 us -> none  [the longest x1 5.68 us: finish_basis(): jnp.einsum('pal,pbl->abl', new_basis, sketch, precision=lax.Precision.HIG...]
    ppermute x4 -> x3, waiting for transfers between devices: 4.29 us -> 14.3 us  [the longest x1 8.7 us: shards(): low = lax.ppermute(coeff, LINE, forward)]
    gather x2 -> x0, local copies, waits for them, and re-layouts: 8.81 us -> none  [near_take(): return jnp.take(extended, local_index, axis=2)]
    unnamed x24 -> x20, local copies, waits for them, and re-layouts: 14.6 us -> 7.3 us
    convert_element_type x3 -> x0, local copies, waits for them, and re-layouts: 7.18 us -> none  [the longest x2 6.04 us: shards(): product = jnp.einsum('etw,ebw->bwt', leaf_basis_matrix, leaf_count_total,...]
    ppermute x2 -> x0, local copies, waits for them, and re-layouts: 4.91 us -> none  [the longest x1 2.46 us: extended_2(): lax.ppermute(lax.slice_in_dim(block, block.shape[dim] - width, None, axis...]
  transfers between devices with their start and end apart: 5 -> 3, of which waited for: 2 -> 3; matrix products, arithmetic and copies ran while one was open for 23% -> 6% of each run, Pallas kernels for 0% -> 0%
where the time goes in v1:
time: 88.9 us; the launch traced here: 87.5 us
  Pallas kernels  51.6 us (58%)
  waiting for transfers between devices  14.3 us (16%)
  local copies, waits for them, and re-layouts  12 us (13%)
  starting transfers between devices  7.71 us (9%)
  other arithmetic  1.17 us (1%)
    pallas_call x1, Pallas kernels, shards(): pl.pallas_call(far_kernel, grid_spec=pltpu.PrefetchScalarGridSpec(num_sca...  30.5 us
    pallas_call x1, Pallas kernels, shards(): pl.pallas_call(coeff_kernel, grid=(steps,), in_specs=[pl.BlockSpec((vecto...  12.8 us
    ppermute x1, waiting for transfers between devices, shards(): low = lax.ppermute(coeff, LINE, forward)  8.7 us
    pallas_call x1, Pallas kernels, shards(): pl.pallas_call(functools.partial(finish_kernel, len(pieces)), in_specs=[p...  8.22 us
    unnamed x20, local copies, waits for them, and re-layouts  7.3 us
    ppermute x1, starting transfers between devices, shards(): low = lax.ppermute(coeff, LINE, forward)  4.49 us
    ppermute x1, waiting for transfers between devices, shards(): pieces = (packed, lax.ppermute(packed, 'vector', [(0, 1), (1, 0)]))  4.19 us
    ppermute x1, starting transfers between devices, shards(): high = lax.ppermute(coeff, LINE, backward)  1.91 us
  transfers between devices with their start and end apart: 3, of which 3 were waited for; matrix products, arithmetic and copies ran while one was open for 6% of the time, Pallas kernels for 0%

profile of v1, /device:TPU:1, one launch (start us, length us, event | category | flops | bytes accessed | tf_op | source)
XLA Modules:
  0.0 87.5 jit_solution(9820379300577999460)
XLA Ops:
  0.6 2.4 %copy.17 = bf16[32,32,128]{1,0,2:T(8,128)(2,1)S(1)} copy(bf16[32,32,128]{2,1,0:T(8,128)(2,1)} %param.10) | data formatting | bytes 524288 | tf_op args[2]
  3.0 0.0 copy-start
  3.0 1.1 %copy.19.down_ref = bf16[64,32,64]{2,1,0:T(8,128)(2,1)} copy(bf16[64,32,64]{1,2,0:T(8,128)(2,1)S(1)} %bitcast.13) | data formatting | bytes 524288 | tf_op jit(solution)/shard_map/reshape | solution.py:175
  4.2 0.0 copy-done
  4.2 2.5 %copy.16 = bf16[32,64,128]{1,0,2:T(8,128)(2,1)} copy(bf16[32,64,128]{2,1,0:T(8,128)(2,1)S(1)} %copy-done) | data formatting | bytes 1048576 | tf_op args[1]
  6.7 12.8 %coefficients.1.own_ref = bf16[64,48,128]{2,1,0:T(8,128)(2,1)} custom-call(bf16[64,8192]{1,0:T(8,128)(2,1)} %samples_ref.1, bf16[128,32,64]{2,1,0:T(8,128)(2,1)} %bitcast.11, bf16[64,32,64]{2,1,0:T(8,128)(2,1)} %copy.19.down_ref), custom_call_target="tpu_custom_call" | custom-call | tf_op jit(solution)/shard_map/coefficients/pallas_call | solution.py:176
  19.5 1.9 %collective-permute-start.1 = (bf16[64,48,128]{2,1,0:T(8,128)(2,1)}, bf16[64,48,128]{2,1,0:T(8,128)(2,1)S(1)}, u32[]{:S(2)}, u32[]{:S(2)}) collective-permute-start(bf16[64,48,128]{2,1,0:T(8,128)(2,1)} %coefficients.1.own_ref), channel_id=1, source_target_pairs={{1,0},{2,1},{3,2},{8,3},{9,8},{10,9},{11,10},{16,11},{17,16},{18,1... | collective-permute-start | bytes 2359304 | tf_op jit(solution)/shard_map/ppermute | solution.py:193
  21.4 4.5 %collective-permute-start = (bf16[64,48,128]{2,1,0:T(8,128)(2,1)}, bf16[64,48,128]{2,1,0:T(8,128)(2,1)}, u32[]{:S(2)}, u32[]{:S(2)}) collective-permute-start(bf16[64,48,128]{2,1,0:T(8,128)(2,1)} %coefficients.1.own_ref), channel_id=1, source_target_pairs={{0,1},{1,2},{2,3},{3,8},{8,9},{9,10},{10,11},{11,16},{16,17},{17,1... | collective-permute-start | bytes 2359304 | tf_op jit(solution)/shard_map/ppermute | solution.py:192
  25.9 0.0 copy-start.5
  25.9 0.7 copy-done.5
  26.6 0.7 copy.25.test_ref
  27.3 0.0 copy-done.1
  27.3 0.2 copy.20
  27.5 0.0 copy-start.2
  27.5 1.7 %copy.22.leaf_coupling_ref = bf16[128,32,128]{2,1,0:T(8,128)(2,1)} copy(bf16[128,32,128]{0,2,1:T(8,128)(2,1)S(1)} %bitcast.14) | data formatting | bytes 2097152 | tf_op jit(solution)/shard_map/reshape | solution.py:198
  29.2 0.0 copy-done.2
  29.2 0.2 copy.21
  29.5 0.0 copy-start.6
  29.5 1.6 %copy.23.parent_coupling_ref = bf16[64,32,128]{2,1,0:T(8,128)(2,1)} copy(bf16[64,32,128]{0,2,1:T(8,128)(2,1)S(1)} %bitcast.15) | data formatting | bytes 1048576 | tf_op jit(solution)/shard_map/reshape | solution.py:199
  31.1 0.0 copy-done.6
  31.1 0.0 copy-start.7
  31.1 0.6 broadcast_subtract_fusion.1.leaf_lists_ref
  31.7 0.1 copy-done.7
  31.8 0.6 broadcast_subtract_fusion.parent_lists_ref
  32.4 1.5 %collective-permute-done.1.high_ref = bf16[64,48,128]{2,1,0:T(8,128)(2,1)S(1)} collective-permute-done((bf16[64,48,128]{2,1,0:T(8,128)(2,1)}, bf16[64,48,128]{2,1,0:T(8,128)(2,1)S(1)}, u32[]{:S(2)}, u32[]{:S(2)}) %collective-permute-start.1) | collective-permute-done | bytes 786464 | tf_op jit(solution)/shard_map/ppermute | solution.py:193
  33.8 8.7 %collective-permute-done.low_ref = bf16[64,48,128]{2,1,0:T(8,128)(2,1)} collective-permute-done((bf16[64,48,128]{2,1,0:T(8,128)(2,1)}, bf16[64,48,128]{2,1,0:T(8,128)(2,1)}, u32[]{:S(2)}, u32[]{:S(2)}) %collective-permute-start) | collective-permute-done | bytes 786464 | tf_op jit(solution)/shard_map/ppermute | solution.py:192
  42.5 0.0 copy-done.3
  42.5 30.5 %far_field.1 = (bf16[64,8192]{1,0:T(8,128)(2,1)}, bf16[1024,128]{1,0:T(8,128)(2,1)}) custom-call(s32[4,128]{1,0:T(4,128)} %broadcast_subtract_fusion.1.leaf_lists_ref, s32[4,64]{1,0:T(4,128)} %broadcast_subtract_fusion.parent_lists_ref, bf16[64,48,128]{2,1,0:T(8,128)(2,1)} %collective-permute-done.low_ref, bf16[64,48,128]{2,1,0:T(8,128)(2,1)} %coefficients.1.own_ref, ...), custom_call_target="tpu_custom_call" | custom-call | tf_op jit(solution)/shard_map/far_field/pallas_call | solution.py:202
  73.1 1.3 %collective-permute-start.2 = (bf16[1024,128]{1,0:T(8,128)(2,1)}, bf16[1024,128]{1,0:T(8,128)(2,1)S(1)}, u32[]{:S(2)}, u32[]{:S(2)}) collective-permute-start(bf16[1024,128]{1,0:T(8,128)(2,1)} %get-tuple-element.8.refs_0_), channel_id=1, source_target_pairs={{0,4},{4,0},{1,5},{5,1},{2,6},{6,2},{3,7},{7,3},{8,12},{12,8},{9,1... | collective-permute-start | bytes 786440 | tf_op jit(solution)/shard_map/ppermute | solution.py:235
  74.4 4.2 %collective-permute-done.2.refs_1_ = bf16[1024,128]{1,0:T(8,128)(2,1)S(1)} collective-permute-done((bf16[1024,128]{1,0:T(8,128)(2,1)}, bf16[1024,128]{1,0:T(8,128)(2,1)S(1)}, u32[]{:S(2)}, u32[]{:S(2)}) %collective-permute-start.2) | collective-permute-done | bytes 262176 | tf_op jit(solution)/shard_map/ppermute | solution.py:235
  78.6 0.7 copy-done.4
  79.3 8.2 %finish.1 = (f32[64,32,128]{2,1,0:T(8,128)}, f32[32,32,128]{2,1,0:T(8,128)}) custom-call(bf16[1024,128]{1,0:T(8,128)(2,1)} %get-tuple-element.8.refs_0_, bf16[1024,128]{1,0:T(8,128)(2,1)} %copy-done.4, bf16[32,64,128]{2,1,0:T(8,128)(2,1)} %refs_2_.1), custom_call_target="tpu_custom_call" | custom-call | tf_op jit(solution)/shard_map/finish/pallas_call | solution.py:238
  (3 shorter events, 0.0 us)
Async XLA Ops:
  3.0 1.1 %copy-start = (bf16[32,64,128]{2,1,0:T(8,128)(2,1)S(1)}, bf16[32,64,128]{2,1,0:T(8,128)(2,1)}, u32[]{:S(2)}) copy-start(bf16[32,64,128]{2,1,0:T(8,128)(2,1)} %refs_2_.1) | copy-start | bytes 1572868
  6.7 20.6 %copy-start.1 = (bf16[32,32,4,128]{3,2,1,0:T(4,128)(2,1)S(1)}, bf16[32,32,4,128]{3,2,1,0:T(4,128)(2,1)}, u32[]{:S(2)}) copy-start(bf16[32,32,4,128]{3,2,1,0:T(4,128)(2,1)} %param.12) | copy-start | bytes 3145732
  19.5 14.4 %collective-permute-start.1 = (bf16[64,48,128]{2,1,0:T(8,128)(2,1)}, bf16[64,48,128]{2,1,0:T(8,128)(2,1)S(1)}, u32[]{:S(2)}, u32[]{:S(2)}) collective-permute-start(bf16[64,48,128]{2,1,0:T(8,128)(2,1)} %coefficients.1.own_ref), channel_id=1, source_target_pairs={{1,0},{2,1},{3,2},{8,3},{9,8},{10,9},{11,10},{16,11},{17,16},{18,1... | collective-permute-start | bytes 2359304 | tf_op jit(solution)/shard_map/ppermute | solution.py:193
  21.4 21.1 %collective-permute-start = (bf16[64,48,128]{2,1,0:T(8,128)(2,1)}, bf16[64,48,128]{2,1,0:T(8,128)(2,1)}, u32[]{:S(2)}, u32[]{:S(2)}) collective-permute-start(bf16[64,48,128]{2,1,0:T(8,128)(2,1)} %coefficients.1.own_ref), channel_id=1, source_target_pairs={{0,1},{1,2},{2,3},{3,8},{8,9},{9,10},{10,11},{11,16},{16,17},{17,1... | collective-permute-start | bytes 2359304 | tf_op jit(solution)/shard_map/ppermute | solution.py:192
  25.9 0.7 copy-start.5
  27.5 1.7 %copy-start.2 = (bf16[32,32,4,64]{3,2,1,0:T(4,128)(2,1)S(1)}, bf16[32,32,4,64]{3,2,1,0:T(4,128)(2,1)}, u32[]{:S(2)}) copy-start(bf16[32,32,4,64]{3,2,1,0:T(4,128)(2,1)} %param.14) | copy-start | bytes 1572868
  29.5 1.7 %copy-start.6 = (s32[4,128]{1,0:T(4,128)S(1)}, s32[4,128]{1,0:T(4,128)}, u32[]{:S(2)}) copy-start(s32[4,128]{1,0:T(4,128)} %param.11) | copy-start | bytes 6148
  31.1 0.7 copy-start.7
  33.8 8.7 %copy-start.3 = (bf16[64,48,128]{2,1,0:T(8,128)(2,1)}, bf16[64,48,128]{2,1,0:T(8,128)(2,1)S(1)}, u32[]{:S(2)}) copy-start(bf16[64,48,128]{2,1,0:T(8,128)(2,1)S(1)} %collective-permute-done.1.high_ref) | copy-start | bytes 2359300
  73.1 5.5 %collective-permute-start.2 = (bf16[1024,128]{1,0:T(8,128)(2,1)}, bf16[1024,128]{1,0:T(8,128)(2,1)S(1)}, u32[]{:S(2)}, u32[]{:S(2)}) collective-permute-start(bf16[1024,128]{1,0:T(8,128)(2,1)} %get-tuple-element.8.refs_0_), channel_id=1, source_target_pairs={{0,4},{4,0},{1,5},{5,1},{2,6},{6,2},{3,7},{7,3},{8,12},{12,8},{9,1... | collective-permute-start | bytes 786440 | tf_op jit(solution)/shard_map/ppermute | solution.py:235
  78.6 0.7 copy-start.4

commit v2 on v1

--- a/solution.py
+++ b/solution.py
@@ -26,15 +26,18 @@
     )
 
 
-def coeff_kernel(samples_ref, basis_ref, down_ref, coeff_ref):
-    count, rank = down_ref.shape[0], down_ref.shape[1]
+def coeff_kernel(samples_ref, basis_ref, up_ref, coeff_ref):
+    count, rank = up_ref.shape[0], basis_ref.shape[1]
     width = 2 * basis_ref.shape[2]
     half = rank // 2
+    leaves = []
     for q in range(count):
         both = block_diagonal((basis_ref[2 * q], basis_ref[2 * q + 1]))
         points = samples_ref[:, q * width : (q + 1) * width]
-        leaf = dot(both, points, NT).astype(BF16)
-        parent = dot(down_ref[q], leaf).astype(BF16)
+        leaves.append(dot(both, points, NT).astype(BF16))
+    parents = [dot(up_ref[q], leaves[q], TN).astype(BF16) for q in range(count)]
+    for q in range(count):
+        leaf, parent = leaves[q], parents[q]
         coeff_ref[q, :rank, :] = jnp.concatenate([leaf[:rank], leaf[rank:]], axis=1)
         coeff_ref[q, rank:, :] = jnp.concatenate([parent[:half], parent[half:]], axis=1)
 
@@ -52,7 +55,7 @@
     high_ref,
     leaf_coupling_ref,
     parent_coupling_ref,
-    down_ref,
+    up_ref,
     basis_ref,
     test_ref,
     product_ref,
@@ -62,7 +65,7 @@
     totals,
 ):
     step = pl.program_id(0)
-    count, rank = down_ref.shape[0], down_ref.shape[1]
+    count, rank = up_ref.shape[0], basis_ref.shape[1]
     vectors = product_ref.shape[0]
     width = 2 * basis_ref.shape[2]
     parents = own_ref.shape[0]
@@ -83,31 +86,38 @@
                     parent_ext[target, : rank // 2, :] = up
                     parent_ext[target, rank // 2 :, :] = swap_halves(up)
 
+    before = lax.axis_index(LINE) - 1
+    leaf_first, parent_first = before * (2 * parents), before * parents
+    leaf_far, parent_far = [], []
     for i in range(count):
         q = step * count + i
-        far = []
         for c in range(2):
-            t = 2 * q + c
             source = jnp.concatenate(
-                [leaf_ext[leaf_lists_ref[k, t]] for k in range(leaf_lists_ref.shape[0])], axis=0
+                [leaf_ext[leaf_lists_ref[k, 2 * q + c] - leaf_first] for k in range(leaf_lists_ref.shape[0])],
+                axis=0,
             )
-            far.append(dot(leaf_coupling_ref[2 * i + c], source))
+            leaf_far.append(dot(leaf_coupling_ref[2 * i + c], source))
         source = jnp.concatenate(
-            [parent_ext[parent_lists_ref[k, q]] for k in range(parent_lists_ref.shape[0])], axis=0
+            [parent_ext[parent_lists_ref[k, q] - parent_first] for k in range(parent_lists_ref.shape[0])], axis=0
         )
-        parent_far = dot(parent_coupling_ref[i], source).astype(BF16)
-        descend = dot(down_ref[i], parent_far, TN)
-        total = (jnp.concatenate(far, axis=0) + descend).astype(BF16)
-        rows = pl.ds(pl.multiple_of(q * 2 * rank, 2 * rank), 2 * rank)
-        totals[rows, :] = total.astype(F32)
+        parent_far.append(dot(parent_coupling_ref[i], source).astype(BF16))
+    descend = [dot(up_ref[i], parent_far[i]) for i in range(count)]
+    total = []
+    for i in range(count):
+        far = jnp.concatenate(leaf_far[2 * i : 2 * i + 2], axis=0)
+        total.append((far + descend[i]).astype(BF16))
+    for i in range(count):
         both = block_diagonal((basis_ref[2 * i], basis_ref[2 * i + 1]))
-        product_ref[:, i * width : (i + 1) * width] = dot(total[:, :vectors], both, TN).astype(BF16)
+        product_ref[:, i * width : (i + 1) * width] = dot(total[i][:, :vectors], both, TN).astype(BF16)
+    for i in range(count):
+        rows = pl.ds(pl.multiple_of((step * count + i) * 2 * rank, 2 * rank), 2 * rank)
+        totals[rows, :] = total[i].astype(F32)
 
     @pl.when(step == pl.num_programs(0) - 1)
     def _():
         for a in range(rank):
             mine = totals[pl.ds(a, 2 * parents, stride=rank), :][:, :vectors].astype(BF16)
-            packed_ref[a * rank : (a + 1) * rank, :] = dot(test_ref[...], mine, (((0,), (1,)), ((), ()))).astype(BF16)
+            packed_ref[a * rank : (a + 1) * rank, :] = dot(test_ref[...], mine, NT).astype(BF16)
 
 
 def finish_kernel(parts, *refs):
@@ -168,23 +178,24 @@
     vectors = samples.shape[0]
     parents = leaves // 2
     leaf_blocks, parent_blocks = leaf_lists.shape[0], parent_lists.shape[0]
-    count = 8
+    count = 16 if parents % 16 == 0 else parents
     steps = parents // count
 
     basis = leaf_basis_matrix.transpose(2, 0, 1)
-    down = transfer.reshape(rank, rank, parents, 2).transpose(2, 1, 3, 0).reshape(parents, rank, 2 * rank)
+    up = transfer.transpose(2, 0, 1).reshape(parents, 2 * rank, rank)
+    test = test_matrix.T
     coeff = pl.pallas_call(
         coeff_kernel,
         grid=(steps,),
         in_specs=[
             pl.BlockSpec((vectors, 2 * count * width), lambda i: (0, i)),
             pl.BlockSpec((2 * count, rank, width), lambda i: (i, 0, 0)),
-            pl.BlockSpec((count, rank, 2 * rank), lambda i: (i, 0, 0)),
+            pl.BlockSpec((count, 2 * rank, rank), lambda i: (i, 0, 0)),
         ],
         out_specs=pl.BlockSpec((count, rank + rank // 2, 2 * vectors), lambda i: (i, 0, 0)),
         out_shape=jax.ShapeDtypeStruct((parents, rank + rank // 2, 2 * vectors), BF16),
         name="coefficients",
-    )(samples, basis, down)
+    )(samples, basis, up)
 
     size = lax.axis_size(LINE)
     forward = [(i, i + 1) for i in range(size - 1)]
@@ -192,9 +203,6 @@
     low = lax.ppermute(coeff, LINE, forward)
     high = lax.ppermute(coeff, LINE, backward)
 
-    position = lax.axis_index(LINE)
-    leaf_local = leaf_lists - (position - 1) * leaves
-    parent_local = parent_lists - (position - 1) * parents
     leaf_mats = leaf_coupling.transpose(3, 0, 2, 1).reshape(leaves, rank, leaf_blocks * rank)
     parent_mats = parent_coupling.transpose(3, 0, 2, 1).reshape(parents, rank, parent_blocks * rank)
 
@@ -210,9 +218,9 @@
                 whole,
                 pl.BlockSpec((2 * count, rank, leaf_blocks * rank), lambda i, *_: (i, 0, 0)),
                 pl.BlockSpec((count, rank, parent_blocks * rank), lambda i, *_: (i, 0, 0)),
-                pl.BlockSpec((count, rank, 2 * rank), lambda i, *_: (i, 0, 0)),
+                pl.BlockSpec((count, 2 * rank, rank), lambda i, *_: (i, 0, 0)),
                 pl.BlockSpec((2 * count, rank, width), lambda i, *_: (i, 0, 0)),
-                pl.BlockSpec(test_matrix.shape, lambda i, *_: (0, 0)),
+                pl.BlockSpec(test.shape, lambda i, *_: (0, 0)),
             ],
             out_specs=[
                 pl.BlockSpec((vectors, 2 * count * width), lambda i, *_: (0, i)),
@@ -229,7 +237,7 @@
             jax.ShapeDtypeStruct((rank * rank, leaves), BF16),
         ],
         name="far_field",
-    )(leaf_local, parent_local, low, coeff, high, leaf_mats, parent_mats, down, basis, test_matrix)
+    )(leaf_lists, parent_lists, low, coeff, high, leaf_mats, parent_mats, up, basis, test)
 
     if lax.axis_size("vector") == 2:
         pieces = (packed, lax.ppermute(packed, "vector", [(0, 1), (1, 0)]))

time: 88.9 us -> 62.8 us (0.71)
  the two profiles are of different devices: /device:TPU:1 before, /device:TPU:10 now
where the time goes in v2:
time: 62.8 us; the launch traced here: 62.4 us
  Pallas kernels  25.7 us (41%)
  waiting for transfers between devices  19.9 us (32%)
  local copies, waits for them, and re-layouts  10.3 us (16%)
  starting transfers between devices  5.89 us (9%)
  between operations  0.69 us (1%)
    pallas_call x1, Pallas kernels, shards(): pl.pallas_call(far_kernel, grid_spec=pltpu.PrefetchScalarGridSpec(num_sca...  12.7 us
    ppermute x1, waiting for transfers between devices, shards(): high = lax.ppermute(coeff, LINE, backward)  12 us
    pallas_call x1, Pallas kernels, shards(): pl.pallas_call(functools.partial(finish_kernel, len(pieces)), in_specs=[p...  8.22 us
    ppermute x1, waiting for transfers between devices, shards(): pieces = (packed, lax.ppermute(packed, 'vector', [(0, 1), (1, 0)]))  5.06 us
    pallas_call x1, Pallas kernels, shards(): pl.pallas_call(coeff_kernel, grid=(steps,), in_specs=[pl.BlockSpec((vecto...  4.71 us
    unnamed x12, local copies, waits for them, and re-layouts  3.44 us
    transpose x1, local copies, waits for them, and re-layouts, shards(): up = transfer.transpose(2, 0, 1).reshape(parents, 2 * rank, rank)  3.28 us
    ppermute x1, waiting for transfers between devices, shards(): low = lax.ppermute(coeff, LINE, forward)  2.8 us
  transfers between devices with their start and end apart: 3, of which 3 were waited for; matrix products, arithmetic and copies ran while one was open for 6% of the time, Pallas kernels for 0%

profile of v2, /device:TPU:10, one launch (start us, length us, event | category | flops | bytes accessed | tf_op | source)
XLA Modules:
  0.0 62.4 jit_solution(8841156323590914732)
XLA Ops:
  0.6 0.0 copy-start
  0.6 3.3 %copy.16 = bf16[128,32,32]{2,1,0:T(8,128)(2,1)} copy(bf16[128,32,32]{0,2,1:T(8,128)(2,1)} %bitcast.16) | data formatting | bytes 524288 | tf_op jit(solution)/shard_map/transpose | solution.py:185
  3.9 0.0 copy-done
  3.9 2.5 %copy.15 = bf16[32,64,128]{1,0,2:T(8,128)(2,1)} copy(bf16[32,64,128]{2,1,0:T(8,128)(2,1)S(1)} %copy-done) | data formatting | bytes 1048576 | tf_op args[1]
  6.4 0.0 copy-start.1
  6.4 4.7 %coefficients.1.own_ref = bf16[64,48,128]{2,1,0:T(8,128)(2,1)} custom-call(bf16[64,8192]{1,0:T(8,128)(2,1)} %samples_ref.1, bf16[128,32,64]{2,1,0:T(8,128)(2,1)} %bitcast.11, bf16[64,64,32]{2,1,0:T(8,128)(2,1)} %bitcast.9), custom_call_target="tpu_custom_call" | custom-call | tf_op jit(solution)/shard_map/coefficients/pallas_call | solution.py:187
  11.1 1.9 %collective-permute-start.1 = (bf16[64,48,128]{2,1,0:T(8,128)(2,1)}, bf16[64,48,128]{2,1,0:T(8,128)(2,1)S(1)}, u32[]{:S(2)}, u32[]{:S(2)}) collective-permute-start(bf16[64,48,128]{2,1,0:T(8,128)(2,1)} %coefficients.1.own_ref), channel_id=1, source_target_pairs={{1,0},{2,1},{3,2},{8,3},{9,8},{10,9},{11,10},{16,11},{17,16},{18,1... | collective-permute-start | bytes 2359304 | tf_op jit(solution)/shard_map/ppermute | solution.py:204
  13.1 2.4 %collective-permute-start = (bf16[64,48,128]{2,1,0:T(8,128)(2,1)}, bf16[64,48,128]{2,1,0:T(8,128)(2,1)}, u32[]{:S(2)}, u32[]{:S(2)}) collective-permute-start(bf16[64,48,128]{2,1,0:T(8,128)(2,1)} %coefficients.1.own_ref), channel_id=1, source_target_pairs={{0,1},{1,2},{2,3},{3,8},{8,9},{9,10},{10,11},{11,16},{16,17},{17,1... | collective-permute-start | bytes 2359304 | tf_op jit(solution)/shard_map/ppermute | solution.py:203
  15.5 0.0 copy-done.1
  15.5 0.2 copy.17
  15.7 0.0 copy-start.2
  15.7 1.7 %copy.19.leaf_coupling_ref = bf16[128,32,128]{2,1,0:T(8,128)(2,1)} copy(bf16[128,32,128]{0,2,1:T(8,128)(2,1)S(1)} %bitcast.13) | data formatting | bytes 2097152 | tf_op jit(solution)/shard_map/reshape | solution.py:206
  17.4 0.0 copy-done.2
  17.4 0.2 copy.18
  17.6 1.6 %copy.20.parent_coupling_ref = bf16[64,32,128]{2,1,0:T(8,128)(2,1)} copy(bf16[64,32,128]{0,2,1:T(8,128)(2,1)S(1)} %bitcast.14) | data formatting | bytes 1048576 | tf_op jit(solution)/shard_map/reshape | solution.py:207
  19.3 12.0 %collective-permute-done.1.high_ref = bf16[64,48,128]{2,1,0:T(8,128)(2,1)S(1)} collective-permute-done((bf16[64,48,128]{2,1,0:T(8,128)(2,1)}, bf16[64,48,128]{2,1,0:T(8,128)(2,1)S(1)}, u32[]{:S(2)}, u32[]{:S(2)}) %collective-permute-start.1) | collective-permute-done | bytes 786464 | tf_op jit(solution)/shard_map/ppermute | solution.py:204
  31.3 0.0 copy-start.3
  31.3 2.8 %collective-permute-done.low_ref = bf16[64,48,128]{2,1,0:T(8,128)(2,1)} collective-permute-done((bf16[64,48,128]{2,1,0:T(8,128)(2,1)}, bf16[64,48,128]{2,1,0:T(8,128)(2,1)}, u32[]{:S(2)}, u32[]{:S(2)}) %collective-permute-start) | collective-permute-done | bytes 786464 | tf_op jit(solution)/shard_map/ppermute | solution.py:203
  34.1 0.0 copy-done.3
  34.1 12.7 %far_field.1 = (bf16[64,8192]{1,0:T(8,128)(2,1)}, bf16[1024,128]{1,0:T(8,128)(2,1)}) custom-call(s32[4,128]{1,0:T(4,128)} %leaf_lists_ref.1, s32[4,64]{1,0:T(4,128)} %parent_lists_ref.1, bf16[64,48,128]{2,1,0:T(8,128)(2,1)} %collective-permute-done.low_ref, bf16[64,48,128]{2,1,0:T(8,128)(2,1)} %coefficients.1.own_ref, bf16[64,48,128]{2,1,0:T(8,128)(2,1)} %copy-done.3, ...), custom_call_target="tpu_custom_call" | custom-call | tf_op jit(solution)/shard_map/far_field/pallas_call | solution.py:210
  46.8 1.6 %collective-permute-start.2 = (bf16[1024,128]{1,0:T(8,128)(2,1)}, bf16[1024,128]{1,0:T(8,128)(2,1)S(1)}, u32[]{:S(2)}, u32[]{:S(2)}) collective-permute-start(bf16[1024,128]{1,0:T(8,128)(2,1)} %get-tuple-element.8.refs_0_), channel_id=1, source_target_pairs={{0,4},{4,0},{1,5},{5,1},{2,6},{6,2},{3,7},{7,3},{8,12},{12,8},{9,1... | collective-permute-start | bytes 786440 | tf_op jit(solution)/shard_map/ppermute | solution.py:243
  48.4 5.1 %collective-permute-done.2.refs_1_ = bf16[1024,128]{1,0:T(8,128)(2,1)S(1)} collective-permute-done((bf16[1024,128]{1,0:T(8,128)(2,1)}, bf16[1024,128]{1,0:T(8,128)(2,1)S(1)}, u32[]{:S(2)}, u32[]{:S(2)}) %collective-permute-start.2) | collective-permute-done | bytes 262176 | tf_op jit(solution)/shard_map/ppermute | solution.py:243
  53.5 0.0 copy-start.4
  53.5 0.7 %copy-done.4 = bf16[1024,128]{1,0:T(8,128)(2,1)} copy-done((bf16[1024,128]{1,0:T(8,128)(2,1)}, bf16[1024,128]{1,0:T(8,128)(2,1)S(1)}, u32[]{:S(2)}) %copy-start.4) | copy-done | bytes 262168
  54.2 8.2 %finish.1 = (f32[64,32,128]{2,1,0:T(8,128)}, f32[32,32,128]{2,1,0:T(8,128)}) custom-call(bf16[1024,128]{1,0:T(8,128)(2,1)} %get-tuple-element.8.refs_0_, bf16[1024,128]{1,0:T(8,128)(2,1)} %copy-done.4, bf16[32,64,128]{2,1,0:T(8,128)(2,1)} %refs_2_.1), custom_call_target="tpu_custom_call" | custom-call | tf_op jit(solution)/shard_map/finish/pallas_call | solution.py:246
Async XLA Ops:
  0.6 3.3 %copy-start = (bf16[32,64,128]{2,1,0:T(8,128)(2,1)S(1)}, bf16[32,64,128]{2,1,0:T(8,128)(2,1)}, u32[]{:S(2)}) copy-start(bf16[32,64,128]{2,1,0:T(8,128)(2,1)} %refs_2_.1) | copy-start | bytes 1572868
  6.4 9.0 %copy-start.1 = (bf16[32,32,4,128]{3,2,1,0:T(4,128)(2,1)S(1)}, bf16[32,32,4,128]{3,2,1,0:T(4,128)(2,1)}, u32[]{:S(2)}) copy-start(bf16[32,32,4,128]{3,2,1,0:T(4,128)(2,1)} %param.12) | copy-start | bytes 3145732
  11.1 20.1 %collective-permute-start.1 = (bf16[64,48,128]{2,1,0:T(8,128)(2,1)}, bf16[64,48,128]{2,1,0:T(8,128)(2,1)S(1)}, u32[]{:S(2)}, u32[]{:S(2)}) collective-permute-start(bf16[64,48,128]{2,1,0:T(8,128)(2,1)} %coefficients.1.own_ref), channel_id=1, source_target_pairs={{1,0},{2,1},{3,2},{8,3},{9,8},{10,9},{11,10},{16,11},{17,16},{18,1... | collective-permute-start | bytes 2359304 | tf_op jit(solution)/shard_map/ppermute | solution.py:204
  13.1 21.0 %collective-permute-start = (bf16[64,48,128]{2,1,0:T(8,128)(2,1)}, bf16[64,48,128]{2,1,0:T(8,128)(2,1)}, u32[]{:S(2)}, u32[]{:S(2)}) collective-permute-start(bf16[64,48,128]{2,1,0:T(8,128)(2,1)} %coefficients.1.own_ref), channel_id=1, source_target_pairs={{0,1},{1,2},{2,3},{3,8},{8,9},{9,10},{10,11},{11,16},{16,17},{17,1... | collective-permute-start | bytes 2359304 | tf_op jit(solution)/shard_map/ppermute | solution.py:203
  15.7 1.7 %copy-start.2 = (bf16[32,32,4,64]{3,2,1,0:T(4,128)(2,1)S(1)}, bf16[32,32,4,64]{3,2,1,0:T(4,128)(2,1)}, u32[]{:S(2)}) copy-start(bf16[32,32,4,64]{3,2,1,0:T(4,128)(2,1)} %param.14) | copy-start | bytes 1572868
  31.3 2.8 %copy-start.3 = (bf16[64,48,128]{2,1,0:T(8,128)(2,1)}, bf16[64,48,128]{2,1,0:T(8,128)(2,1)S(1)}, u32[]{:S(2)}) copy-start(bf16[64,48,128]{2,1,0:T(8,128)(2,1)S(1)} %collective-permute-done.1.high_ref) | copy-start | bytes 2359300
  46.8 6.6 %collective-permute-start.2 = (bf16[1024,128]{1,0:T(8,128)(2,1)}, bf16[1024,128]{1,0:T(8,128)(2,1)S(1)}, u32[]{:S(2)}, u32[]{:S(2)}) collective-permute-start(bf16[1024,128]{1,0:T(8,128)(2,1)} %get-tuple-element.8.refs_0_), channel_id=1, source_target_pairs={{0,4},{4,0},{1,5},{5,1},{2,6},{6,2},{3,7},{7,3},{8,12},{12,8},{9,1... | collective-permute-start | bytes 786440 | tf_op jit(solution)/shard_map/ppermute | solution.py:243
  53.5 0.7 %copy-start.4 = (bf16[1024,128]{1,0:T(8,128)(2,1)}, bf16[1024,128]{1,0:T(8,128)(2,1)S(1)}, u32[]{:S(2)}) copy-start(bf16[1024,128]{1,0:T(8,128)(2,1)S(1)} %collective-permute-done.2.refs_1_) | copy-start | bytes 786436

commit v3 on v1

v3 whole, which is shorter than its diff:
```python
import functools

import jax
import jax.numpy as jnp
from jax import lax
from jax.experimental import pallas as pl
from jax.experimental.pallas import tpu as pltpu
from jax.sharding import PartitionSpec as P

F32 = jnp.float32
BF16 = jnp.bfloat16
LINE = ("cluster", "replica")
TN = (((0,), (0,)), ((), ()))
NT = (((1,), (1,)), ((), ()))


def dot(a, b, dims=(((1,), (0,)), ((), ()))):
    return lax.dot_general(a, b, dims, preferred_element_type=F32)


def block_diagonal(pair):
    first, second = pair[0], pair[1]
    zero = jnp.zeros_like(first)
    return jnp.concatenate(
        [jnp.concatenate([first, zero], axis=1), jnp.concatenate([zero, second], axis=1)], axis=0
    )


def swap_halves(block):
    half = block.shape[1] // 2
    return jnp.concatenate([block[:, half:], block[:, :half]], axis=1)


def near(source, first, count):
    return jnp.minimum(jnp.maximum(source - first, 0), count - 1)


def sources_kernel(
    group,
    leaf_lists_ref,
    parent_lists_ref,
    samples_ref,
    basis_ref,
    up_ref,
    leaf_coupling_ref,
    parent_coupling_ref,
    test_ref,
    product_ref,
    packed_ref,
    coeff,
    leaf_ext,
    parent_ext,
    totals,
    leaf_mats,
    parent_mats,
    send_sem,
    recv_sem,
):
    parents, rank = up_ref.shape[0], basis_ref.shape[1]
    leaves = 2 * parents
    vectors = product_ref.shape[0]
    width = 2 * basis_ref.shape[2]
    half = rank // 2
    chunks = parents // group
    leaf_blocks, parent_blocks = leaf_lists_ref.shape[0], parent_lists_ref.shape[0]

    replicas = lax.axis_size("replica")
    size = lax.axis_size("cluster") * replicas
    here = lax.axis_index("cluster") * replicas + lax.axis_index("replica")
    vector = lax.axis_index("vector")

    def device(place):
        return (place // replicas, vector, lax.rem(place, replicas))

    right = device(lax.rem(here + 1, size))
    left = device(lax.rem(here + size - 1, size))

    barrier = pltpu.get_barrier_semaphore()
    for neighbour in (left, right):
        pl.semaphore_signal(barrier, inc=1, device_id=neighbour, device_id_type=pl.DeviceIdType.MESH)
    pl.semaphore_wait(barrier, 2)

    def copies(chunk):
        rows = pl.ds(chunk * group, group)
        return [
            pltpu.make_async_remote_copy(
                src_ref=coeff.at[1, rows],
                dst_ref=coeff.at[slot, rows],
                send_sem=send_sem.at[way, chunk],
                recv_sem=recv_sem.at[way, chunk],
                device_id=target,
                device_id_type=pl.DeviceIdType.MESH,
            )
            for way, (slot, target) in enumerate(((0, right), (2, left)))
        ]

    def coefficients(chunk, carry):
        leaf, parent = [], []
        for j in range(group):
            q = chunk * group + j
            both = block_diagonal((basis_ref[2 * q], basis_ref[2 * q + 1]))
            points = samples_ref[:, pl.ds(pl.multiple_of(q * width, width), width)]
            leaf.append(dot(both, points, NT).astype(BF16))
        for j in range(group):
            parent.append(dot(up_ref[chunk * group + j], leaf[j], TN).astype(BF16))
        for j in range(group):
            q = chunk * group + j
            coeff[1, q, :rank, :] = jnp.concatenate([leaf[j][:rank], leaf[j][rank:]], axis=1)
            coeff[1, q, rank:, :] = jnp.concatenate([parent[j][:half], parent[j][half:]], axis=1)
        for copy in copies(chunk):
            copy.start()
        return carry

    lax.fori_loop(0, chunks, coefficients, 0)

    def relayout(block, carry):
        for u in range(4):
            r = block * 4 + u
            leaf_mats[pl.ds(r, leaves, stride=rank), :] = leaf_coupling_ref[r].astype(F32).T
            parent_mats[pl.ds(r, parents, stride=rank), :] = parent_coupling_ref[r].astype(F32).T
        return carry

    lax.fori_loop(0, rank // 4, relayout, 0)

    def unpack(place, first, many):
        def some(block, carry):
            for u in range(8):
                q = first + block * 8 + u
                target = place * parents + q
                pair = coeff[place, q, :rank, :]
                up = coeff[place, q, rank:, :]
                leaf_ext[2 * target] = pair
                leaf_ext[2 * target + 1] = swap_halves(pair)
                parent_ext[target, :half, :] = up
                parent_ext[target, half:, :] = swap_halves(up)
            return carry

        lax.fori_loop(0, many // 8, some, 0)

    unpack(1, 0, parents)

    def arrive(chunk, carry):
        for copy, place in zip(copies(chunk), (0, 2)):
            copy.wait()
            unpack(place, chunk * group, group)
        return carry

    lax.fori_loop(0, chunks, arrive, 0)

    leaf_first, parent_first = (here - 1) * leaves, (here - 1) * parents

    def far_field(chunk, carry):
        leaf_far, parent_far, total = [], [], []
        for j in range(group):
            q = chunk * group + j
            for c in range(2):
                t = 2 * q + c
                source = jnp.concatenate(
                    [leaf_ext[near(leaf_lists_ref[k, t], leaf_first, 3 * leaves)] for k in range(leaf_blocks)], axis=0
                )
                mats = leaf_mats[pl.ds(pl.multiple_of(t * rank, rank), rank), :].astype(BF16)
                leaf_far.append(dot(mats, source))
            source = jnp.concatenate(
                [parent_ext[near(parent_lists_ref[k, q], parent_first, 3 * parents)] for k in range(parent_blocks)],
                axis=0,
            )
            mats = parent_mats[pl.ds(pl.multiple_of(q * rank, rank), rank), :].astype(BF16)
            parent_far.append(dot(mats, source).astype(BF16))
        descend = [dot(up_ref[chunk * group + j], parent_far[j]) for j in range(group)]
        for j in range(group):
            far = jnp.concatenate(leaf_far[2 * j : 2 * j + 2], axis=0)
            total.append((far + descend[j]).astype(BF16))
        for j in range(group):
            q = chunk * group + j
            both = block_diagonal((basis_ref[2 * q], basis_ref[2 * q + 1]))
            columns = pl.ds(pl.multiple_of(q * width, width), width)
            product_ref[:, columns] = dot(total[j][:, :vectors], both, TN).astype(BF16)
        for j in range(group):
            q = chunk * group + j
            totals[pl.ds(pl.multiple_of(q * 2 * rank, 2 * rank), 2 * rank), :] = total[j].astype(F32)
        return carry

    lax.fori_loop(0, chunks, far_field, 0)

    def pack(block, carry):
        for u in range(8):
            a = block * 8 + u
            mine = totals[pl.ds(a, leaves, stride=rank), :][:, :vectors].astype(BF16)
            rows = pl.ds(pl.multiple_of(a * rank, rank), rank)
            packed_ref[rows, :] = dot(test_ref[...], mine, NT).astype(BF16)
        return carry

    lax.fori_loop(0, rank // 8, pack, 0)


def finish_kernel(parts, *refs):
    basis_ref, new_basis_ref, fresh_ref, summed, wide, sketch = refs[parts:]
    rank, width = basis_ref.shape[0], basis_ref.shape[1]
    lanes = basis_ref.shape[2]
    total = refs[0][...].astype(F32)
    for ref in refs[1:parts]:
        total = total + ref[...].astype(F32)
    summed[...] = total
    for a in range(rank):
        wide[a * width : (a + 1) * width, :] = basis_ref[a].astype(F32)
    group = 8

    def points(block, square):
        first = block * group
        acc = [jnp.zeros((rank, lanes), F32) for _ in range(group)]
        for a in range(rank):
            mixed = summed[a * rank : (a + 1) * rank, :]
            for j in range(group):
                acc[j] = acc[j] + wide[pl.ds(a * width + first + j, 1), :] * mixed
        for j in range(group):
            sketch[first + j] = acc[j]
            square = square + acc[j] * acc[j]
        return square

    square = lax.fori_loop(0, width // group, points, jnp.zeros((rank, lanes), F32))
    scale = lax.rsqrt(square / width + 1e-06)
    for p in range(width):
        new_basis_ref[p] = sketch[p] * scale

    def grams(block, carry):
        first = block * group

        acc = [jnp.zeros((rank, lanes), F32) for _ in range(group)]
        for p in range(width):
            row = sketch[p]
            for j in range(group):
                acc[j] = acc[j] + new_basis_ref[p, pl.ds(first + j, 1), :] * row
        for j in range(group):
            fresh_ref[first + j] = acc[j] / width
        return carry

    lax.fori_loop(0, rank // group, grams, 0)


def shards(
    samples,
    leaf_basis_matrix,
    transfer,
    leaf_lists,
    leaf_coupling,
    parent_lists,
    parent_coupling,
    test_matrix,
):
    rank, width, leaves = leaf_basis_matrix.shape
    vectors = samples.shape[0]
    parents = leaves // 2
    leaf_blocks, parent_blocks = leaf_lists.shape[0], parent_lists.shape[0]
    group = 16 if parents % 16 == 0 else parents
    chunks = parents // group
    leaf_sums, parent_sums = leaf_blocks * rank, parent_blocks * rank

    basis = leaf_basis_matrix.transpose(2, 0, 1)
    up = transfer.transpose(2, 0, 1).reshape(parents, 2 * rank, rank)
    test = test_matrix.T
    leaf_blocks_first = leaf_coupling.transpose(0, 2, 1, 3).reshape(rank, leaf_sums, leaves)
    parent_blocks_first = parent_coupling.transpose(0, 2, 1, 3).reshape(rank, parent_sums, parents)

    product, packed = pl.pallas_call(
        functools.partial(sources_kernel, group),
        in_specs=[pl.BlockSpec(memory_space=pltpu.SMEM)] * 2 + [pl.BlockSpec(memory_space=pltpu.VMEM)] * 6,
        out_specs=[pl.BlockSpec(memory_space=pltpu.VMEM)] * 2,
        out_shape=[
            jax.ShapeDtypeStruct(samples.shape, BF16),
            jax.ShapeDtypeStruct((rank * rank, leaves), BF16),
        ],
        scratch_shapes=[
            pltpu.VMEM((3, parents, rank + rank // 2, 2 * vectors), BF16),
            pltpu.VMEM((3 * leaves, rank, 2 * vectors), BF16),
            pltpu.VMEM((3 * parents, rank, 2 * vectors), BF16),
            pltpu.VMEM((leaves * rank, 2 * vectors), F32),
            pltpu.VMEM((leaves * rank, leaf_sums), F32),
            pltpu.VMEM((parents * rank, parent_sums), F32),
            pltpu.SemaphoreType.DMA((2, chunks)),
            pltpu.SemaphoreType.DMA((2, chunks)),
        ],
        compiler_params=pltpu.CompilerParams(collective_id=0, has_side_effects=True),
        name="far_field",
    )(leaf_lists, parent_lists, samples, basis, up, leaf_blocks_first, parent_blocks_first, test)

    if lax.axis_size("vector") == 2:
        pieces = (packed, lax.ppermute(packed, "vector", [(0, 1), (1, 0)]))
    else:
        pieces = (lax.psum(packed.astype(F32), "vector"),)
    new_basis, fresh = pl.pallas_call(
        functools.partial(finish_kernel, len(pieces)),
        in_specs=[pl.BlockSpec(memory_space=pltpu.VMEM)] * (len(pieces) + 1),
        out_specs=[pl.BlockSpec(memory_space=pltpu.VMEM)] * 2,
        out_shape=[
            jax.ShapeDtypeStruct((width, rank, leaves), F32),
            jax.ShapeDtypeStruct((rank, rank, leaves), F32),
        ],
        scratch_shapes=[
            pltpu.VMEM((rank * rank, leaves), F32),
            pltpu.VMEM((rank * width, leaves), F32),
            pltpu.VMEM((width, rank, leaves), F32),
        ],
        name="finish",
    )(*pieces, leaf_basis_matrix)
    return product, new_basis, fresh


def solution(mesh):
    placed = (
        P("vector", LINE),
        P(None, None, LINE),
        P(None, None, LINE),
        P(None, LINE),
        P(None, None, None, LINE),
        P(None, LINE),
        P(None, None, None, LINE),
        P("vector", None),
    )
    return jax.shard_map(
        shards,
        mesh=mesh,
        in_specs=placed,
        out_specs=(P("vector", LINE), P(None, None, LINE), P(None, None, LINE)),
        check_vma=False,
    )
```

time: 88.9 us -> 56 us (0.63)
  Pallas kernels: 51.6 us -> 39 us
  waiting for transfers between devices: 14.3 us -> 4.19 us
  starting transfers between devices: 7.71 us -> 1.31 us
  local copies, waits for them, and re-layouts: 12 us -> 10.2 us
  other arithmetic: 1.17 us -> 0 us
    pallas_call x2 -> x1, Pallas kernels: 43.3 us -> 30.8 us  [shards(): pl.pallas_call(functools.partial(sources_kernel, group), in_specs=[pl.Blo...]
    ppermute x2 -> x0, waiting for transfers between devices: 10.2 us -> none  [the longest x1 8.7 us: shards(): low = lax.ppermute(coeff, LINE, forward)]
    ppermute x2 -> x0, starting transfers between devices: 6.41 us -> none  [the longest x1 4.49 us: shards(): low = lax.ppermute(coeff, LINE, forward)]
    transpose x1 -> x3, local copies, waits for them, and re-layouts: 0.22 us -> 5.75 us  [the longest x1 3.32 us: shards(): up = transfer.transpose(2, 0, 1).reshape(parents, 2 * rank, rank)]
    reshape x3 -> x0, local copies, waits for them, and re-layouts: 4.48 us -> none  [the longest x1 1.7 us: shards(): leaf_coupling.transpose(3, 0, 2, 1)]
    unnamed x20 -> x12, local copies, waits for them, and re-layouts: 7.3 us -> 4.42 us
    sub x2 -> x0, other arithmetic: 1.17 us -> none  [the longest x1 0.6 us: shards(): leaf_local = leaf_lists - (position - 1) * leaves]
  transfers between devices with their start and end apart: 3 -> 1, of which waited for: 3 -> 1; matrix products, arithmetic and copies ran while one was open for 6% -> 0% of each run, Pallas kernels for 0% -> 0%
where the time goes in v3:
time: 56 us; the launch traced here: 55.3 us
  Pallas kernels  39 us (70%)
  local copies, waits for them, and re-layouts  10.2 us (18%)
  waiting for transfers between devices  4.19 us (7%)
  starting transfers between devices  1.31 us (2%)
  between operations  0.66 us (1%)
    pallas_call x1, Pallas kernels, shards(): pl.pallas_call(functools.partial(sources_kernel, group), in_specs=[pl.Blo...  30.8 us
    pallas_call x1, Pallas kernels, shards(): pl.pallas_call(functools.partial(finish_kernel, len(pieces)), in_specs=[p...  8.22 us
    unnamed x12, local copies, waits for them, and re-layouts  4.42 us
    ppermute x1, waiting for transfers between devices, shards(): pieces = (packed, lax.ppermute(packed, 'vector', [(0, 1), (1, 0)]))  4.19 us
    transpose x1, local copies, waits for them, and re-layouts, shards(): up = transfer.transpose(2, 0, 1).reshape(parents, 2 * rank, rank)  3.32 us
    ppermute x1, starting transfers between devices, shards(): pieces = (packed, lax.ppermute(packed, 'vector', [(0, 1), (1, 0)]))  1.31 us
    transpose x1, local copies, waits for them, and re-layouts, shards(): parent_coupling.transpose(0, 2, 1, 3).reshape(rank, parent_sums, parents)  1.25 us
    transpose x1, local copies, waits for them, and re-layouts, shards(): leaf_coupling.transpose(0, 2, 1, 3).reshape(rank, leaf_sums, leaves)  1.18 us
  transfers between devices with their start and end apart: 1, of which 1 were waited for; matrix products, arithmetic and copies ran while one was open for 0% of the time, Pallas kernels for 0%

profile of v3, /device:TPU:1, one launch (start us, length us, event | category | flops | bytes accessed | tf_op | source)
XLA Modules:
  0.0 55.3 jit_solution(4627710133111386894)
XLA Ops:
  0.6 0.0 copy-start.1
  0.6 3.3 %copy.12 = bf16[128,32,32]{2,1,0:T(8,128)(2,1)} copy(bf16[128,32,32]{0,2,1:T(8,128)(2,1)} %bitcast.14) | data formatting | bytes 524288 | tf_op jit(solution)/shard_map/transpose | solution.py:259
  4.0 0.0 copy-done.1
  4.0 0.0 copy-start.2
  4.0 1.2 %copy.13 = bf16[32,4,32,128]{3,2,1,0:T(8,128)(2,1)} copy(bf16[32,4,32,128]{3,1,2,0:T(4,128)(2,1)S(1)} %bitcast.12) | data formatting | bytes 2097152 | tf_op jit(solution)/shard_map/transpose | solution.py:261
  5.1 0.2 copy-done.2
  5.4 0.0 copy-start
  5.4 1.2 %copy.14 = bf16[32,4,32,64]{3,2,1,0:T(8,128)(2,1)} copy(bf16[32,4,32,64]{3,1,2,0:T(4,128)(2,1)S(1)} %bitcast.13) | data formatting | bytes 1048576 | tf_op jit(solution)/shard_map/transpose | solution.py:262
  6.6 0.0 copy-done
  6.6 2.5 %copy.11 = bf16[32,64,128]{1,0,2:T(8,128)(2,1)} copy(bf16[32,64,128]{2,1,0:T(8,128)(2,1)S(1)} %copy-done) | data formatting | bytes 1048576 | tf_op args[1]
  9.1 30.8 %far_field.1 = (bf16[64,8192]{1,0:T(8,128)(2,1)}, bf16[1024,128]{1,0:T(8,128)(2,1)}) custom-call(s32[4,128]{1,0:T(4,128)} %leaf_lists_ref.1, s32[4,64]{1,0:T(4,128)} %parent_lists_ref.1, bf16[64,8192]{1,0:T(8,128)(2,1)} %samples_ref.1, bf16[128,32,64]{2,1,0:T(8,128)(2,1)} %bitcast.11, bf16[64,64,32]{2,1,0:T(8,128)(2,1)} %bitcast.8, ...), custom_call_target="tpu_custom_call" | custom-call | tf_op jit(solution)/shard_map/far_field/pallas_call | solution.py:264
  39.9 0.0 copy-start.3
  39.9 1.3 %collective-permute-start = (bf16[1024,128]{1,0:T(8,128)(2,1)}, bf16[1024,128]{1,0:T(8,128)(2,1)S(1)}, u32[]{:S(2)}, u32[]{:S(2)}) collective-permute-start(bf16[1024,128]{1,0:T(8,128)(2,1)} %get-tuple-element.8.refs_0_), channel_id=1, source_target_pairs={{0,4},{4,0},{1,5},{5,1},{2,6},{6,2},{3,7},{7,3},{8,12},{12,8},{9,1... | collective-permute-start | bytes 786440 | tf_op jit(solution)/shard_map/ppermute | solution.py:287
  41.2 4.2 %collective-permute-done.refs_1_ = bf16[1024,128]{1,0:T(8,128)(2,1)S(1)} collective-permute-done((bf16[1024,128]{1,0:T(8,128)(2,1)}, bf16[1024,128]{1,0:T(8,128)(2,1)S(1)}, u32[]{:S(2)}, u32[]{:S(2)}) %collective-permute-start) | collective-permute-done | bytes 262176 | tf_op jit(solution)/shard_map/ppermute | solution.py:287
  45.4 0.0 copy-start.4
  45.4 0.7 %copy-done.4 = bf16[1024,128]{1,0:T(8,128)(2,1)} copy-done((bf16[1024,128]{1,0:T(8,128)(2,1)}, bf16[1024,128]{1,0:T(8,128)(2,1)S(1)}, u32[]{:S(2)}) %copy-start.4) | copy-done | bytes 262168
  46.1 8.2 %finish.1 = (f32[64,32,128]{2,1,0:T(8,128)}, f32[32,32,128]{2,1,0:T(8,128)}) custom-call(bf16[1024,128]{1,0:T(8,128)(2,1)} %get-tuple-element.8.refs_0_, bf16[1024,128]{1,0:T(8,128)(2,1)} %copy-done.4, bf16[32,64,128]{2,1,0:T(8,128)(2,1)} %refs_2_.1), custom_call_target="tpu_custom_call" | custom-call | tf_op jit(solution)/shard_map/finish/pallas_call | solution.py:290
  54.4 0.0 copy-done.3
  54.4 1.0 %copy.16 = bf16[64,8192]{1,0:T(8,128)(2,1)} copy(bf16[64,8192]{1,0:T(8,128)(2,1)S(1)} %copy-done.3) | data formatting | bytes 2097152
Async XLA Ops:
  0.6 3.3 %copy-start.1 = (bf16[32,32,4,128]{3,2,1,0:T(4,128)(2,1)S(1)}, bf16[32,32,4,128]{3,2,1,0:T(4,128)(2,1)}, u32[]{:S(2)}) copy-start(bf16[32,32,4,128]{3,2,1,0:T(4,128)(2,1)} %param.12) | copy-start | bytes 3145732
  4.0 1.4 %copy-start.2 = (bf16[32,32,4,64]{3,2,1,0:T(4,128)(2,1)S(1)}, bf16[32,32,4,64]{3,2,1,0:T(4,128)(2,1)}, u32[]{:S(2)}) copy-start(bf16[32,32,4,64]{3,2,1,0:T(4,128)(2,1)} %param.14) | copy-start | bytes 1572868
  5.4 1.3 %copy-start = (bf16[32,64,128]{2,1,0:T(8,128)(2,1)S(1)}, bf16[32,64,128]{2,1,0:T(8,128)(2,1)}, u32[]{:S(2)}) copy-start(bf16[32,64,128]{2,1,0:T(8,128)(2,1)} %refs_2_.1) | copy-start | bytes 1572868
  39.9 14.4 %copy-start.3 = (bf16[64,8192]{1,0:T(8,128)(2,1)S(1)}, bf16[64,8192]{1,0:T(8,128)(2,1)}, u32[]{:S(2)}) copy-start(bf16[64,8192]{1,0:T(8,128)(2,1)} %get-tuple-element.14) | copy-start | bytes 3145732
  39.9 5.5 %collective-permute-start = (bf16[1024,128]{1,0:T(8,128)(2,1)}, bf16[1024,128]{1,0:T(8,128)(2,1)S(1)}, u32[]{:S(2)}, u32[]{:S(2)}) collective-permute-start(bf16[1024,128]{1,0:T(8,128)(2,1)} %get-tuple-element.8.refs_0_), channel_id=1, source_target_pairs={{0,4},{4,0},{1,5},{5,1},{2,6},{6,2},{3,7},{7,3},{8,12},{12,8},{9,1... | collective-permute-start | bytes 786440 | tf_op jit(solution)/shard_map/ppermute | solution.py:287
  45.4 0.7 %copy-start.4 = (bf16[1024,128]{1,0:T(8,128)(2,1)}, bf16[1024,128]{1,0:T(8,128)(2,1)S(1)}, u32[]{:S(2)}) copy-start(bf16[1024,128]{1,0:T(8,128)(2,1)S(1)} %collective-permute-done.refs_1_) | copy-start | bytes 786436

commit v4 on v3

--- a/solution.py
+++ b/solution.py
@@ -31,6 +31,11 @@
     return jnp.concatenate([block[:, half:], block[:, :half]], axis=1)
 
 
+def blocks_first(block):
+    sources, blocks, targets = block.shape
+    return jnp.swapaxes(block.astype(F32), 0, 1).reshape(blocks * sources, targets).T
+
+
 def near(source, first, count):
     return jnp.minimum(jnp.maximum(source - first, 0), count - 1)
 
@@ -41,25 +46,31 @@
     parent_lists_ref,
     samples_ref,
     basis_ref,
-    up_ref,
+    transfer_ref,
     leaf_coupling_ref,
     parent_coupling_ref,
     test_ref,
     product_ref,
-    packed_ref,
+    summed_ref,
     coeff,
+    mats,
     leaf_ext,
     parent_ext,
     totals,
     leaf_mats,
     parent_mats,
+    own_packed,
+    peer_packed,
     send_sem,
     recv_sem,
+    packed_send_sem,
+    packed_recv_sem,
 ):
-    parents, rank = up_ref.shape[0], basis_ref.shape[1]
-    leaves = 2 * parents
+    rank, each, leaves = basis_ref.shape
+    parents = leaves // 2
     vectors = product_ref.shape[0]
-    width = 2 * basis_ref.shape[2]
+    width = 2 * each
+    paired = lax.axis_size("vector") == 2
     half = rank // 2
     chunks = parents // group
     leaf_blocks, parent_blocks = leaf_lists_ref.shape[0], parent_lists_ref.shape[0]
@@ -76,9 +87,30 @@
     left = device(lax.rem(here + size - 1, size))
 
     barrier = pltpu.get_barrier_semaphore()
-    for neighbour in (left, right):
+    peer = (lax.axis_index("cluster"), 1 - vector, lax.axis_index("replica"))
+    greeted = (left, right, peer) if paired else (left, right)
+    for neighbour in greeted:
         pl.semaphore_signal(barrier, inc=1, device_id=neighbour, device_id_type=pl.DeviceIdType.MESH)
-    pl.semaphore_wait(barrier, 2)
+
+    def by_leaf(block, carry):
+        for u in range(4):
+            r = block * 4 + u
+            both = jnp.concatenate([basis_ref[r], transfer_ref[r]], axis=0).astype(F32)
+            mats[pl.ds(r, leaves, stride=rank), :] = both.T
+        return carry
+
+    lax.fori_loop(0, rank // 4, by_leaf, 0)
+    pl.semaphore_wait(barrier, len(greeted))
+
+    def pair_of(q):
+        return mats[pl.ds(pl.multiple_of(q * 2 * rank, 2 * rank), 2 * rank), :].astype(BF16)
+
+    def bases(q):
+        pair = pair_of(q)[:, :each]
+        return block_diagonal((pair[:rank], pair[rank:]))
+
+    def lift(q):
+        return pair_of(q)[:, each:]
 
     def copies(chunk):
         rows = pl.ds(chunk * group, group)
@@ -94,15 +126,24 @@
             for way, (slot, target) in enumerate(((0, right), (2, left)))
         ]
 
+    def packed_copy(chunk):
+        return pltpu.make_async_remote_copy(
+            src_ref=own_packed.at[chunk],
+            dst_ref=peer_packed.at[chunk],
+            send_sem=packed_send_sem.at[chunk],
+            recv_sem=packed_recv_sem.at[chunk],
+            device_id=peer,
+            device_id_type=pl.DeviceIdType.MESH,
+        )
+
     def coefficients(chunk, carry):
         leaf, parent = [], []
         for j in range(group):
             q = chunk * group + j
-            both = block_diagonal((basis_ref[2 * q], basis_ref[2 * q + 1]))
             points = samples_ref[:, pl.ds(pl.multiple_of(q * width, width), width)]
-            leaf.append(dot(both, points, NT).astype(BF16))
-        for j in range(group):
-            parent.append(dot(up_ref[chunk * group + j], leaf[j], TN).astype(BF16))
+            leaf.append(dot(bases(q), points, NT).astype(BF16))
+        for j in range(group):
+            parent.append(dot(lift(chunk * group + j), leaf[j], TN).astype(BF16))
         for j in range(group):
             q = chunk * group + j
             coeff[1, q, :rank, :] = jnp.concatenate([leaf[j][:rank], leaf[j][rank:]], axis=1)
@@ -116,8 +157,8 @@
     def relayout(block, carry):
         for u in range(4):
             r = block * 4 + u
-            leaf_mats[pl.ds(r, leaves, stride=rank), :] = leaf_coupling_ref[r].astype(F32).T
-            parent_mats[pl.ds(r, parents, stride=rank), :] = parent_coupling_ref[r].astype(F32).T
+            leaf_mats[pl.ds(r, leaves, stride=rank), :] = blocks_first(leaf_coupling_ref[r])
+            parent_mats[pl.ds(r, parents, stride=rank), :] = blocks_first(parent_coupling_ref[r])
         return carry
 
     lax.fori_loop(0, rank // 4, relayout, 0)
@@ -166,41 +207,47 @@
             )
             mats = parent_mats[pl.ds(pl.multiple_of(q * rank, rank), rank), :].astype(BF16)
             parent_far.append(dot(mats, source).astype(BF16))
-        descend = [dot(up_ref[chunk * group + j], parent_far[j]) for j in range(group)]
+        descend = [dot(lift(chunk * group + j), parent_far[j]) for j in range(group)]
         for j in range(group):
             far = jnp.concatenate(leaf_far[2 * j : 2 * j + 2], axis=0)
             total.append((far + descend[j]).astype(BF16))
         for j in range(group):
             q = chunk * group + j
-            both = block_diagonal((basis_ref[2 * q], basis_ref[2 * q + 1]))
             columns = pl.ds(pl.multiple_of(q * width, width), width)
-            product_ref[:, columns] = dot(total[j][:, :vectors], both, TN).astype(BF16)
+            product_ref[:, columns] = dot(total[j][:, :vectors], bases(q), TN).astype(BF16)
         for j in range(group):
             q = chunk * group + j
             totals[pl.ds(pl.multiple_of(q * 2 * rank, 2 * rank), 2 * rank), :] = total[j].astype(F32)
+        first = chunk * (group * 2 * rank)
+        for block in range(rank // chunks):
+            mine = jnp.concatenate(
+                [totals[pl.ds(first + block * chunks + j, 2 * group, stride=rank), :] for j in range(chunks)], axis=0
+            )
+            mine = mine[:, :vectors].astype(BF16)
+            own_packed[chunk, block * rank : (block + 1) * rank, :] = dot(test_ref[...], mine, NT).astype(BF16)
+        if paired:
+            packed_copy(chunk).start()
         return carry
 
     lax.fori_loop(0, chunks, far_field, 0)
 
-    def pack(block, carry):
-        for u in range(8):
-            a = block * 8 + u
-            mine = totals[pl.ds(a, leaves, stride=rank), :][:, :vectors].astype(BF16)
-            rows = pl.ds(pl.multiple_of(a * rank, rank), rank)
-            packed_ref[rows, :] = dot(test_ref[...], mine, NT).astype(BF16)
-        return carry
-
-    lax.fori_loop(0, rank // 8, pack, 0)
-
-
-def finish_kernel(parts, *refs):
-    basis_ref, new_basis_ref, fresh_ref, summed, wide, sketch = refs[parts:]
+    if paired:
+        for chunk in range(chunks):
+            packed_copy(chunk).wait()
+    for block in range(rank // chunks):
+        rows = slice(block * rank, (block + 1) * rank)
+        parts = [own_packed[chunk, rows, :].astype(F32) for chunk in range(chunks)]
+        if paired:
+            parts = [parts[chunk] + peer_packed[chunk, rows, :].astype(F32) for chunk in range(chunks)]
+        for j in range(chunks):
+            lanes = slice(j * 2 * group, (j + 1) * 2 * group)
+            a = block * chunks + j
+            summed_ref[a * rank : (a + 1) * rank, :] = jnp.concatenate([part[:, lanes] for part in parts], axis=1)
+
+
+def finish_kernel(summed, basis_ref, new_basis_ref, fresh_ref, wide, sketch):
     rank, width = basis_ref.shape[0], basis_ref.shape[1]
     lanes = basis_ref.shape[2]
-    total = refs[0][...].astype(F32)
-    for ref in refs[1:parts]:
-        total = total + ref[...].astype(F32)
-    summed[...] = total
     for a in range(rank):
         wide[a * width : (a + 1) * width, :] = basis_ref[a].astype(F32)
     group = 8
@@ -255,53 +302,50 @@
     chunks = parents // group
     leaf_sums, parent_sums = leaf_blocks * rank, parent_blocks * rank
 
-    basis = leaf_basis_matrix.transpose(2, 0, 1)
-    up = transfer.transpose(2, 0, 1).reshape(parents, 2 * rank, rank)
     test = test_matrix.T
-    leaf_blocks_first = leaf_coupling.transpose(0, 2, 1, 3).reshape(rank, leaf_sums, leaves)
-    parent_blocks_first = parent_coupling.transpose(0, 2, 1, 3).reshape(rank, parent_sums, parents)
-
-    product, packed = pl.pallas_call(
+    product, summed = pl.pallas_call(
         functools.partial(sources_kernel, group),
         in_specs=[pl.BlockSpec(memory_space=pltpu.SMEM)] * 2 + [pl.BlockSpec(memory_space=pltpu.VMEM)] * 6,
         out_specs=[pl.BlockSpec(memory_space=pltpu.VMEM)] * 2,
         out_shape=[
             jax.ShapeDtypeStruct(samples.shape, BF16),
-            jax.ShapeDtypeStruct((rank * rank, leaves), BF16),
+            jax.ShapeDtypeStruct((rank * rank, leaves), F32),
         ],
         scratch_shapes=[
             pltpu.VMEM((3, parents, rank + rank // 2, 2 * vectors), BF16),
+            pltpu.VMEM((leaves * rank, width + rank), F32),
             pltpu.VMEM((3 * leaves, rank, 2 * vectors), BF16),
             pltpu.VMEM((3 * parents, rank, 2 * vectors), BF16),
             pltpu.VMEM((leaves * rank, 2 * vectors), F32),
             pltpu.VMEM((leaves * rank, leaf_sums), F32),
             pltpu.VMEM((parents * rank, parent_sums), F32),
+            pltpu.VMEM((chunks, rank // chunks * rank, leaves), BF16),
+            pltpu.VMEM((chunks, rank // chunks * rank, leaves), BF16),
             pltpu.SemaphoreType.DMA((2, chunks)),
             pltpu.SemaphoreType.DMA((2, chunks)),
+            pltpu.SemaphoreType.DMA((chunks,)),
+            pltpu.SemaphoreType.DMA((chunks,)),
         ],
         compiler_params=pltpu.CompilerParams(collective_id=0, has_side_effects=True),
         name="far_field",
-    )(leaf_lists, parent_lists, samples, basis, up, leaf_blocks_first, parent_blocks_first, test)
-
-    if lax.axis_size("vector") == 2:
-        pieces = (packed, lax.ppermute(packed, "vector", [(0, 1), (1, 0)]))
-    else:
-        pieces = (lax.psum(packed.astype(F32), "vector"),)
+    )(leaf_lists, parent_lists, samples, leaf_basis_matrix, transfer, leaf_coupling, parent_coupling, test)
+
+    if lax.axis_size("vector") != 2:
+        summed = lax.psum(summed, "vector")
     new_basis, fresh = pl.pallas_call(
-        functools.partial(finish_kernel, len(pieces)),
-        in_specs=[pl.BlockSpec(memory_space=pltpu.VMEM)] * (len(pieces) + 1),
+        finish_kernel,
+        in_specs=[pl.BlockSpec(memory_space=pltpu.VMEM)] * 2,
         out_specs=[pl.BlockSpec(memory_space=pltpu.VMEM)] * 2,
         out_shape=[
             jax.ShapeDtypeStruct((width, rank, leaves), F32),
             jax.ShapeDtypeStruct((rank, rank, leaves), F32),
         ],
         scratch_shapes=[
-            pltpu.VMEM((rank * rank, leaves), F32),
             pltpu.VMEM((rank * width, leaves), F32),
             pltpu.VMEM((width, rank, leaves), F32),
         ],
         name="finish",
-    )(*pieces, leaf_basis_matrix)
+    )(summed, leaf_basis_matrix)
     return product, new_basis, fresh
 
 

time: 56 us -> 44.8 us (0.80)
  local copies, waits for them, and re-layouts: 10.2 us -> 0.97 us
  waiting for transfers between devices: 4.19 us -> 0 us
  Pallas kernels: 39 us -> 43.1 us
  starting transfers between devices: 1.31 us -> 0 us
    transpose x3 -> x0, local copies, waits for them, and re-layouts: 5.75 us -> none  [the longest x1 3.32 us: shards(): up = transfer.transpose(2, 0, 1).reshape(parents, 2 * rank, rank)]
    ppermute x1 -> x0, waiting for transfers between devices: 4.19 us -> none  [shards(): pieces = (packed, lax.ppermute(packed, 'vector', [(0, 1), (1, 0)]))]
    pallas_call x1, Pallas kernels: 30.8 us -> 34.7 us  [shards(): pl.pallas_call(functools.partial(sources_kernel, group), in_specs=[pl.Blo...]
    unnamed x12 -> x3, local copies, waits for them, and re-layouts: 4.42 us -> 0.97 us
    ppermute x1 -> x0, starting transfers between devices: 1.31 us -> none  [shards(): pieces = (packed, lax.ppermute(packed, 'vector', [(0, 1), (1, 0)]))]
  transfers between devices with their start and end apart: 1 -> 0, of which waited for: 1 -> 0; matrix products, arithmetic and copies ran while one was open for 0% -> 0% of each run, Pallas kernels for 0% -> 0%
where the time goes in v4:
time: 44.8 us; the launch traced here: 44.7 us
  Pallas kernels  43.1 us (96%)
  local copies, waits for them, and re-layouts  0.97 us (2%)
  between operations  0.65 us (1%)
    pallas_call x1, Pallas kernels, shards(): pl.pallas_call(functools.partial(sources_kernel, group), in_specs=[pl.Blo...  34.7 us
    pallas_call x1, Pallas kernels, shards(): pl.pallas_call(finish_kernel, in_specs=[pl.BlockSpec(memory_space=pltpu.V...  8.41 us
    unnamed x3, local copies, waits for them, and re-layouts  0.97 us

profile of v4, /device:TPU:1, one launch (start us, length us, event | category | flops | bytes accessed | tf_op | source)
XLA Modules:
  0.0 44.7 jit_solution(9123122354186410951)
XLA Ops:
  0.6 34.7 %far_field.1 = (bf16[64,8192]{1,0:T(8,128)(2,1)}, f32[1024,128]{1,0:T(8,128)}) custom-call(s32[4,128]{1,0:T(4,128)} %leaf_lists_ref.1, s32[4,64]{1,0:T(4,128)} %parent_lists_ref.1, bf16[64,8192]{1,0:T(8,128)(2,1)} %samples_ref.1, bf16[32,64,128]{2,1,0:T(8,128)(2,1)} %basis_ref.3, bf16[32,32,128]{2,1,0:T(8,128)(2,1)} %transfer_ref.1, ...), custom_call_target="tpu_custom_call" | custom-call | tf_op jit(solution)/shard_map/far_field/pallas_call | solution.py:306
  35.3 0.0 copy-start
  35.3 8.4 %finish.1 = (f32[64,32,128]{2,1,0:T(8,128)}, f32[32,32,128]{2,1,0:T(8,128)}) custom-call(f32[1024,128]{1,0:T(8,128)} %get-tuple-element.8.summed, bf16[32,64,128]{2,1,0:T(8,128)(2,1)} %basis_ref.3), custom_call_target="tpu_custom_call" | custom-call | tf_op jit(solution)/shard_map/finish/pallas_call | solution.py:335
  43.7 0.0 copy-done
  43.7 1.0 %copy.12 = bf16[64,8192]{1,0:T(8,128)(2,1)} copy(bf16[64,8192]{1,0:T(8,128)(2,1)S(1)} %copy-done) | data formatting | bytes 2097152
Async XLA Ops:
  35.3 8.4 %copy-start = (bf16[64,8192]{1,0:T(8,128)(2,1)S(1)}, bf16[64,8192]{1,0:T(8,128)(2,1)}, u32[]{:S(2)}) copy-start(bf16[64,8192]{1,0:T(8,128)(2,1)} %get-tuple-element.14) | copy-start | bytes 3145732

commit v5 on v4

--- a/solution.py
+++ b/solution.py
@@ -112,19 +112,16 @@
     def lift(q):
         return pair_of(q)[:, each:]
 
-    def copies(chunk):
+    def line_copy(way, chunk):
         rows = pl.ds(chunk * group, group)
-        return [
-            pltpu.make_async_remote_copy(
-                src_ref=coeff.at[1, rows],
-                dst_ref=coeff.at[slot, rows],
-                send_sem=send_sem.at[way, chunk],
-                recv_sem=recv_sem.at[way, chunk],
-                device_id=target,
-                device_id_type=pl.DeviceIdType.MESH,
-            )
-            for way, (slot, target) in enumerate(((0, right), (2, left)))
-        ]
+        return pltpu.make_async_remote_copy(
+            src_ref=coeff.at[1, rows],
+            dst_ref=coeff.at[2 * way, rows],
+            send_sem=send_sem.at[way, chunk],
+            recv_sem=recv_sem.at[way, chunk],
+            device_id=(right, left)[way],
+            device_id_type=pl.DeviceIdType.MESH,
+        )
 
     def packed_copy(chunk):
         return pltpu.make_async_remote_copy(
@@ -136,7 +133,7 @@
             device_id_type=pl.DeviceIdType.MESH,
         )
 
-    def coefficients(chunk, carry):
+    def coefficients(chunk):
         leaf, parent = [], []
         for j in range(group):
             q = chunk * group + j
@@ -148,11 +145,21 @@
             q = chunk * group + j
             coeff[1, q, :rank, :] = jnp.concatenate([leaf[j][:rank], leaf[j][rank:]], axis=1)
             coeff[1, q, rank:, :] = jnp.concatenate([parent[j][:half], parent[j][half:]], axis=1)
-        for copy in copies(chunk):
-            copy.start()
-        return carry
-
-    lax.fori_loop(0, chunks, coefficients, 0)
+
+    orders = (list(range(chunks))[::-1], list(range(chunks)))
+    ready, sent = set(), [0, 0]
+    for turn in range(chunks):
+        chunk = turn // 2 if turn % 2 else chunks - 1 - turn // 2
+        coefficients(chunk)
+        ready.add(chunk)
+        progress = True
+        while progress:
+            progress = False
+            for way in range(2):
+                if sent[way] < chunks and orders[way][sent[way]] in ready:
+                    line_copy(way, orders[way][sent[way]]).start()
+                    sent[way] += 1
+                    progress = True
 
     def relayout(block, carry):
         for u in range(4):
@@ -179,14 +186,6 @@
         lax.fori_loop(0, many // 8, some, 0)
 
     unpack(1, 0, parents)
-
-    def arrive(chunk, carry):
-        for copy, place in zip(copies(chunk), (0, 2)):
-            copy.wait()
-            unpack(place, chunk * group, group)
-        return carry
-
-    lax.fori_loop(0, chunks, arrive, 0)
 
     leaf_first, parent_first = (here - 1) * leaves, (here - 1) * parents
 
@@ -229,7 +228,16 @@
             packed_copy(chunk).start()
         return carry
 
-    lax.fori_loop(0, chunks, far_field, 0)
+    arrived = 0
+    for reach in range(chunks // 2 + 1, chunks + 1):
+        for turn in range(arrived, reach):
+            for way in range(2):
+                chunk = orders[way][turn]
+                line_copy(way, chunk).wait()
+                unpack(2 * way, chunk * group, group)
+        arrived = reach
+        low, high = chunks - reach, reach - 1
+        lax.fori_loop(0, 1 if low == high else 2, lambda i, c: far_field(low + i * (high - low), c), 0)
 
     if paired:
         for chunk in range(chunks):

time: 44.8 us -> 43.9 us (0.980)
  Pallas kernels: 43.1 us -> 42.2 us
    pallas_call x1, Pallas kernels: 34.7 us -> 33.7 us  [shards(): pl.pallas_call(functools.partial(sources_kernel, group), in_specs=[pl.Blo...]
where the time goes in v5:
time: 43.9 us; the launch traced here: 43.8 us
  Pallas kernels  42.2 us (96%)
  local copies, waits for them, and re-layouts  0.97 us (2%)
  between operations  0.65 us (1%)
    pallas_call x1, Pallas kernels, shards(): pl.pallas_call(functools.partial(sources_kernel, group), in_specs=[pl.Blo...  33.7 us
    pallas_call x1, Pallas kernels, shards(): pl.pallas_call(finish_kernel, in_specs=[pl.BlockSpec(memory_space=pltpu.V...  8.41 us
    unnamed x3, local copies, waits for them, and re-layouts  0.97 us

profile of v5, /device:TPU:1, one launch (start us, length us, event | category | flops | bytes accessed | tf_op | source)
XLA Modules:
  0.0 43.8 jit_solution(13686296087751308636)
XLA Ops:
  0.6 33.7 %far_field.1 = (bf16[64,8192]{1,0:T(8,128)(2,1)}, f32[1024,128]{1,0:T(8,128)}) custom-call(s32[4,128]{1,0:T(4,128)} %leaf_lists_ref.1, s32[4,64]{1,0:T(4,128)} %parent_lists_ref.1, bf16[64,8192]{1,0:T(8,128)(2,1)} %samples_ref.1, bf16[32,64,128]{2,1,0:T(8,128)(2,1)} %basis_ref.3, bf16[32,32,128]{2,1,0:T(8,128)(2,1)} %transfer_ref.1, ...), custom_call_target="tpu_custom_call" | custom-call | tf_op jit(solution)/shard_map/far_field/pallas_call | solution.py:314
  34.4 0.0 copy-start
  34.4 8.4 %finish.1 = (f32[64,32,128]{2,1,0:T(8,128)}, f32[32,32,128]{2,1,0:T(8,128)}) custom-call(f32[1024,128]{1,0:T(8,128)} %get-tuple-element.8.summed, bf16[32,64,128]{2,1,0:T(8,128)(2,1)} %basis_ref.3), custom_call_target="tpu_custom_call" | custom-call | tf_op jit(solution)/shard_map/finish/pallas_call | solution.py:343
  42.8 0.0 copy-done
  42.8 1.0 %copy.12 = bf16[64,8192]{1,0:T(8,128)(2,1)} copy(bf16[64,8192]{1,0:T(8,128)(2,1)S(1)} %copy-done) | data formatting | bytes 2097152
Async XLA Ops:
  34.4 8.4 %copy-start = (bf16[64,8192]{1,0:T(8,128)(2,1)S(1)}, bf16[64,8192]{1,0:T(8,128)(2,1)}, u32[]{:S(2)}) copy-start(bf16[64,8192]{1,0:T(8,128)(2,1)} %get-tuple-element.14) | copy-start | bytes 3145732

commit v6 on v5

--- a/solution.py
+++ b/solution.py
@@ -253,7 +253,7 @@
             summed_ref[a * rank : (a + 1) * rank, :] = jnp.concatenate([part[:, lanes] for part in parts], axis=1)
 
 
-def finish_kernel(summed, basis_ref, new_basis_ref, fresh_ref, wide, sketch):
+def finish_kernel(summed, basis_ref, new_basis_ref, fresh_ref, wide, sketch, scales, inverses):
     rank, width = basis_ref.shape[0], basis_ref.shape[1]
     lanes = basis_ref.shape[2]
     for a in range(rank):
@@ -277,19 +277,31 @@
     for p in range(width):
         new_basis_ref[p] = sketch[p] * scale
 
-    def grams(block, carry):
+    scales[...] = scale
+    inverses[...] = jnp.sqrt(square / width + 1e-06)
+    for block in range(rank // group):
         first = block * group
 
-        acc = [jnp.zeros((rank, lanes), F32) for _ in range(group)]
-        for p in range(width):
-            row = sketch[p]
-            for j in range(group):
-                acc[j] = acc[j] + new_basis_ref[p, pl.ds(first + j, 1), :] * row
-        for j in range(group):
-            fresh_ref[first + j] = acc[j] / width
-        return carry
-
-    lax.fori_loop(0, rank // group, grams, 0)
+        def grams(part, acc):
+            acc = list(acc)
+            for u in range(group):
+                p = part * group + u
+                row = sketch[p, first:, :]
+                for j in range(group):
+                    acc[j] = acc[j] + new_basis_ref[p, first + j : first + j + 1, :] * row
+            return tuple(acc)
+
+        start = tuple(jnp.zeros((rank - first, lanes), F32) for _ in range(group))
+        acc = lax.fori_loop(0, width // group, grams, start)
+        later = first + group
+        for j in range(group):
+            a = first + j
+            here = acc[j] / width
+            fresh_ref[a, first:, :] = here
+            if later < rank:
+                turned = here[group:] * scales[later:, :] * inverses[a : a + 1, :]
+                flat = fresh_ref.reshape(rank * rank, lanes)
+                flat[pl.ds(later * rank + a, rank - later, stride=rank), :] = turned
 
 
 def shards(
@@ -351,6 +363,8 @@
         scratch_shapes=[
             pltpu.VMEM((rank * width, leaves), F32),
             pltpu.VMEM((width, rank, leaves), F32),
+            pltpu.VMEM((rank, leaves), F32),
+            pltpu.VMEM((rank, leaves), F32),
         ],
         name="finish",
     )(summed, leaf_basis_matrix)

time: 43.9 us -> 42.8 us (0.975)
  Pallas kernels: 42.2 us -> 41.1 us
    pallas_call x1, Pallas kernels: 8.41 us -> 7.31 us  [shards(): pl.pallas_call(finish_kernel, in_specs=[pl.BlockSpec(memory_space=pltpu.V...]
where the time goes in v6:
time: 42.8 us; the launch traced here: 42.7 us
  Pallas kernels  41.1 us (96%)
  local copies, waits for them, and re-layouts  0.97 us (2%)
  between operations  0.65 us (2%)
    pallas_call x1, Pallas kernels, shards(): pl.pallas_call(functools.partial(sources_kernel, group), in_specs=[pl.Blo...  33.7 us
    pallas_call x1, Pallas kernels, shards(): pl.pallas_call(finish_kernel, in_specs=[pl.BlockSpec(memory_space=pltpu.V...  7.31 us
    unnamed x3, local copies, waits for them, and re-layouts  0.97 us

profile of v6, /device:TPU:1, one launch (start us, length us, event | category | flops | bytes accessed | tf_op | source)
XLA Modules:
  0.0 42.7 jit_solution(8500462185380200663)
XLA Ops:
  0.6 33.7 %far_field.1 = (bf16[64,8192]{1,0:T(8,128)(2,1)}, f32[1024,128]{1,0:T(8,128)}) custom-call(s32[4,128]{1,0:T(4,128)} %leaf_lists_ref.1, s32[4,64]{1,0:T(4,128)} %parent_lists_ref.1, bf16[64,8192]{1,0:T(8,128)(2,1)} %samples_ref.1, bf16[32,64,128]{2,1,0:T(8,128)(2,1)} %basis_ref.3, bf16[32,32,128]{2,1,0:T(8,128)(2,1)} %transfer_ref.1, ...), custom_call_target="tpu_custom_call" | custom-call | tf_op jit(solution)/shard_map/far_field/pallas_call | solution.py:326
  34.4 0.0 copy-start
  34.4 7.3 %finish.1 = (f32[64,32,128]{2,1,0:T(8,128)}, f32[32,32,128]{2,1,0:T(8,128)}) custom-call(f32[1024,128]{1,0:T(8,128)} %get-tuple-element.8.summed, bf16[32,64,128]{2,1,0:T(8,128)(2,1)} %basis_ref.3), custom_call_target="tpu_custom_call" | custom-call | tf_op jit(solution)/shard_map/finish/pallas_call | solution.py:355
  41.7 0.0 copy-done
  41.7 1.0 %copy.12 = bf16[64,8192]{1,0:T(8,128)(2,1)} copy(bf16[64,8192]{1,0:T(8,128)(2,1)S(1)} %copy-done) | data formatting | bytes 2097152
Async XLA Ops:
  34.4 7.3 %copy-start = (bf16[64,8192]{1,0:T(8,128)(2,1)S(1)}, bf16[64,8192]{1,0:T(8,128)(2,1)}, u32[]{:S(2)}) copy-start(bf16[64,8192]{1,0:T(8,128)(2,1)} %get-tuple-element.14) | copy-start | bytes 3145732
